TPU v7x, 256 devices: a whole 4x4x8 slice. The times are simulated.
256 devices in a mesh: gx: 4 (over x), gy: 8 (over y, core), gz: 8 (over z).
Axes of the slice: x: 4, y: 4, z: 8, core: 2. Of those that a mesh axis runs over, the one named last changes fastest.
Arguments:
- right_side: float32 [128, 128, 1024], P('gx', 'gy', 'gz'), may hold values from -24 to 24
- conductivity: float32 [128, 128, 1024], P('gx', 'gy', 'gz'), may hold values from 0.2 to 5
Outputs:
- solution: float32 [128, 128, 1024], P('gx', 'gy', 'gz')
- final_residual: float32 [128, 128, 1024], P('gx', 'gy', 'gz')
All inputs are finite; a program needn't handle non-finite values.
Results may differ from a plain program's by a relative error of at most 0.0003.
Values sent between devices are 32-bit elements; how exact they have to be, the bound alone decides.
A program may use at most 64 MiB of HBM per device.

v0:
```python
import jax
import jax.numpy as jnp
from jax import lax
from jax.experimental import pallas as pl
from jax.experimental.pallas import tpu as pltpu
from jax.sharding import PartitionSpec as P

STEPS = 3
COARSE_STEPS = 8
LOWER_EDGE = 0.3
UPPER_EDGE = 2.0
MESH = pl.DeviceIdType.MESH
LANES = 128
EXCHANGES = 8


def chebyshev_factors(sweeps):
    centre_value = 0.5 * (UPPER_EDGE + LOWER_EDGE)
    half_width = 0.5 * (UPPER_EDGE - LOWER_EDGE)
    ratio_value = centre_value / half_width
    damping = 1.0 / ratio_value
    factors = [(0.0, 1.0 / centre_value)]
    for _ in range(1, sweeps):
        damping_next = 1.0 / (2.0 * ratio_value - damping)
        factors.append((damping_next * damping, 2.0 * damping_next / half_width))
        damping = damping_next
    return factors


def up8(value):
    return -(-value // 8) * 8


class Level:
    def __init__(self, index, nx, ny, nz, shared):
        self.index, self.nx, self.ny, self.nz, self.shared = index, nx, ny, nz, shared
        self.pitch = ny + 2
        self.c0 = up8(self.pitch + 1)
        self.n = up8(nx * self.pitch)
        self.rows = 2 * self.c0 + self.n
        self.zo = 0 if nz == LANES else 1
        self.factor = 0.25**index
        self.wide = nz == LANES and not shared
        if self.wide:
            self.first, self.chunks = self.c0, self.n // 8
        else:
            self.first, self.chunks = 0, self.rows // 8
        self.half = -(-self.chunks // 2) if self.wide else self.chunks

    def scratch(self):
        field = pltpu.VMEM((self.n, LANES), jnp.float32)
        padded = pltpu.VMEM((self.rows, LANES), jnp.float32)
        shapes = {name: field for name in ("xm", "xp", "ym", "yp", "zm", "zp", "dg", "iv", "r", "u", "k")}
        shapes.update({name: padded for name in ("d0", "d1", "v")})
        if not self.shared:
            for name in ("s", "q"):
                shapes[name + "x"] = pltpu.VMEM((EXCHANGES, 2, up8(self.ny), LANES), jnp.float32)
                shapes[name + "y"] = pltpu.VMEM((EXCHANGES, 2, up8(self.nx + 2 * self.zo), LANES), jnp.float32)
            zrows = 16 if self.wide else 8
            shapes["sz"] = pltpu.VMEM((EXCHANGES, zrows, LANES), jnp.float32)
            shapes["qz"] = pltpu.VMEM((EXCHANGES, 2, zrows, LANES), jnp.float32)
            shapes["send"] = pltpu.SemaphoreType.DMA((EXCHANGES, 6))
            shapes["recv"] = pltpu.SemaphoreType.DMA((EXCHANGES, 6))
        return shapes

    def groups(self):
        count = -(-self.n // 96)
        size = up8(-(-self.n // count))
        return [(lo, min(size, self.n - lo)) for lo in range(0, self.n, size)]


def dot(a, b):
    return jnp.dot(a, b, precision=lax.Precision.HIGHEST, preferred_element_type=jnp.float32)


def iota(shape, dim):
    return lax.broadcasted_iota(jnp.int32, shape, dim)


def roll(value, shift):
    shift %= LANES
    return pltpu.roll(value, shift, 1) if shift else value


def build(mesh_shape, box):
    gxn, gyn, gzn = mesh_shape
    bx, by, bz = box
    local = [Level(i, bx >> i, by >> i, bz >> i, False) for i in range(3)]
    cx, cy, cz = bx >> 3, by >> 3, bz >> 3
    three = Level(3, gxn * cx, gyn * cy, gzn * cz, True)
    four = Level(4, three.nx // 2, three.ny // 2, three.nz // 2, True)
    levels = local + [three, four]
    blk = cx * cy
    names = [(lv.index, name) for lv in levels for name in lv.scratch()]
    shapes = [shape for lv in levels for shape in lv.scratch().values()]
    extra = {
        "t": pltpu.VMEM((max(lv.rows for lv in levels), LANES), jnp.float32),
        "te": pltpu.VMEM((max(lv.n for lv in levels[1:]) + 16, LANES), jnp.float32),
        "to": pltpu.VMEM((max(lv.n for lv in levels[1:]) + 16, LANES), jnp.float32),
        "half": pltpu.VMEM((128, LANES), jnp.float32),
        "zs": pltpu.VMEM((2, blk, LANES), jnp.float32),
        "zr": pltpu.VMEM((2, gzn, blk, LANES), jnp.float32),
        "ps": pltpu.VMEM((2, blk, LANES), jnp.float32),
        "pr": pltpu.VMEM((2, gxn * gyn, blk, LANES), jnp.float32),
        "zsend": pltpu.SemaphoreType.DMA((2, gzn)),
        "zrecv": pltpu.SemaphoreType.DMA((2, gzn)),
        "psend": pltpu.SemaphoreType.DMA((2, gxn * gyn)),
        "precv": pltpu.SemaphoreType.DMA((2, gxn * gyn)),
    }
    names += [(None, name) for name in extra]
    shapes += list(extra.values())

    def kernel(b_ref, k_ref, u_ref, res_ref, *scratch):
        ref = {key: value for key, value in zip(names, scratch)}
        gx, gy, gz = lax.axis_index("gx"), lax.axis_index("gy"), lax.axis_index("gz")
        has = (gx > 0, gx < gxn - 1, gy > 0, gy < gyn - 1, gz > 0, gz < gzn - 1)
        peer = (
            (gx - 1, gy, gz),
            (gx + 1, gy, gz),
            (gx, gy - 1, gz),
            (gx, gy + 1, gz),
            (gx, gy, gz - 1),
            (gx, gy, gz + 1),
        )
        lane = iota((8, LANES), 1)
        plane_peers = [(i, j) for i in range(gxn) for j in range(gyn) if i or j]

        def plane_peer(i, j):
            return lax.rem(gx + i, gxn), lax.rem(gy + j, gyn)

        def depth_peer(k):
            return lax.rem(gz + k, gzn)

        for lv in levels:
            for name in ("d0", "d1", "v"):
                ref[lv.index, name][...] = jnp.zeros((lv.rows, LANES), jnp.float32)
            if not lv.shared:
                for name in ("qx", "qy", "qz", "sx", "sy"):
                    target = ref[lv.index, name]
                    target[...] = jnp.zeros(target.shape, jnp.float32)

        barrier = pltpu.get_barrier_semaphore()
        for i, j in plane_peers:
            px, py = plane_peer(i, j)
            pl.semaphore_signal(barrier, inc=1, device_id=(px, py, gz), device_id_type=MESH)
        for k in range(1, gzn):
            pl.semaphore_signal(barrier, inc=1, device_id=(gx, gy, depth_peer(k)), device_id_type=MESH)

        counters = [0, 0, 0]

        def link(lv, slot, way):
            axis, side = "xyz"[way // 2], way % 2
            source = ref[lv.index, "s" + axis].at[slot]
            if axis != "z":
                source = source.at[side]
            return pltpu.make_async_remote_copy(
                src_ref=source,
                dst_ref=ref[lv.index, "q" + axis].at[slot, 1 - side],
                send_sem=ref[lv.index, "send"].at[slot, way],
                recv_sem=ref[lv.index, "recv"].at[slot, way ^ 1],
                device_id=peer[way],
                device_id_type=MESH,
            )

        def incoming(lv, slot, way):
            axis, side = "xyz"[way // 2], way % 2
            source = ref[lv.index, "s" + axis].at[slot]
            if axis != "z":
                source = source.at[side]
            return pltpu.make_async_remote_copy(
                src_ref=source,
                dst_ref=ref[lv.index, "q" + axis].at[slot, side],
                send_sem=ref[lv.index, "send"].at[slot, way],
                recv_sem=ref[lv.index, "recv"].at[slot, way],
                device_id=peer[way],
                device_id_type=MESH,
            )

        def start(lv, slot, ways):
            for way in ways:

                @pl.when(has[way])
                def _():
                    link(lv, slot, way).start()

        def finish(lv, slot, ways):
            for way in ways:

                @pl.when(has[way])
                def _():
                    incoming(lv, slot, way).wait_recv()

        def stage_x(lv, buf, slot):
            out = ref[lv.index, "sx"]
            out[slot, 0, pl.ds(0, lv.ny), :] = buf[pl.ds(lv.c0 + 1, lv.ny), :]
            out[slot, 1, pl.ds(0, lv.ny), :] = buf[pl.ds(lv.c0 + (lv.nx - 1) * lv.pitch + 1, lv.ny), :]

        def place_x(lv, buf, slot):
            got = ref[lv.index, "qx"]
            buf[pl.ds(lv.c0 - lv.pitch + 1, lv.ny), :] = got[slot, 0, pl.ds(0, lv.ny), :]
            buf[pl.ds(lv.c0 + lv.nx * lv.pitch + 1, lv.ny), :] = got[slot, 1, pl.ds(0, lv.ny), :]

        def y_span(lv, wide):
            return lv.c0 - wide * lv.pitch, lv.nx + 2 * wide

        def stage_y(lv, buf, slot, wide):
            base, count = y_span(lv, wide)
            out = ref[lv.index, "sy"]
            out[slot, 0, pl.ds(0, count), :] = buf[pl.ds(base + 1, count, stride=lv.pitch), :]
            out[slot, 1, pl.ds(0, count), :] = buf[pl.ds(base + lv.ny, count, stride=lv.pitch), :]

        def place_y(lv, buf, slot, wide):
            base, count = y_span(lv, wide)
            got = ref[lv.index, "qy"]
            buf[pl.ds(base, count, stride=lv.pitch), :] = got[slot, 0, pl.ds(0, count), :]
            buf[pl.ds(base + lv.pitch - 1, count, stride=lv.pitch), :] = got[slot, 1, pl.ds(0, count), :]

        def stage_z(lv, buf, slot):
            out = ref[lv.index, "sz"]
            packed = jnp.zeros((8, LANES), jnp.float32)
            for c in range(lv.chunks):
                cc = c % lv.half
                value = buf[pl.ds(lv.first + 8 * c, 8), :]
                if lv.wide:
                    packed = jnp.where(lane >= 2 * cc, roll(value, 2 * cc + 1), packed)
                else:
                    mine = (lane == 1 + 2 * cc) | (lane == lv.nz + 2 * cc)
                    packed = jnp.where(mine, roll(value, 2 * cc), packed)
                if cc == lv.half - 1 or c == lv.chunks - 1:
                    out[slot, pl.ds(8 * (c // lv.half), 8), :] = packed

        def place_z(lv, buf, slot):
            got = ref[lv.index, "qz"]
            if lv.wide:
                even = lane % 2 == 0
                return [
                    jnp.where(even, got[slot, 0, pl.ds(8 * h, 8), :], roll(got[slot, 1, pl.ds(8 * h, 8), :], -2))
                    for h in range(2)
                ]
            merged = jnp.where(
                lane <= lv.nz, roll(got[slot, 0], -lv.nz), roll(got[slot, 1], lv.nz)
            )
            edge = (lane == 0) | (lane == lv.nz + 1)
            for c in range(lv.chunks):
                span = pl.ds(8 * c, 8)
                buf[span, :] = jnp.where(edge, roll(merged, -2 * c), buf[span, :])
            return None

        def begin_faces(lv, buf):
            slot = counters[lv.index]
            counters[lv.index] += 1
            stage_x(lv, buf, slot)
            start(lv, slot, (0, 1))
            stage_y(lv, buf, slot, 0)
            start(lv, slot, (2, 3))
            stage_z(lv, buf, slot)
            start(lv, slot, (4, 5))
            return slot

        def end_faces(lv, buf, slot):
            finish(lv, slot, range(6))
            place_x(lv, buf, slot)
            place_y(lv, buf, slot, 0)
            return place_z(lv, buf, slot)

        def faces(lv, buf):
            if lv.shared:
                return None
            return end_faces(lv, buf, begin_faces(lv, buf))

        def corners(lv, buf):
            slot = counters[lv.index]
            counters[lv.index] += 1
            stage_x(lv, buf, slot)
            start(lv, slot, (0, 1))
            finish(lv, slot, (0, 1))
            place_x(lv, buf, slot)
            stage_y(lv, buf, slot, 1)
            start(lv, slot, (2, 3))
            finish(lv, slot, (2, 3))
            place_y(lv, buf, slot, 1)
            stage_z(lv, buf, slot)
            start(lv, slot, (4, 5))
            finish(lv, slot, (4, 5))
            place_z(lv, buf, slot)

        def sides(lv, mid, lo, rows, halo):
            below, above = roll(mid, 1), roll(mid, -1)
            if lv.wide:
                edge = jnp.concatenate(
                    [
                        roll(halo[c // lv.half], -2 * (c % lv.half))
                        for c in range(lo // 8, (lo + rows) // 8)
                    ],
                    axis=0,
                )
                where = iota((rows, LANES), 1)
                below = jnp.where(where == 0, edge, below)
                above = jnp.where(where == LANES - 1, edge, above)
            return below, above

        def around(lv, buf, lo, rows, halo):
            base = lv.c0 + lo
            mid = buf[pl.ds(base, rows), :]
            below, above = sides(lv, mid, lo, rows, halo)
            return mid, (
                buf[pl.ds(base - lv.pitch, rows), :],
                buf[pl.ds(base + lv.pitch, rows), :],
                buf[pl.ds(base - 1, rows), :],
                buf[pl.ds(base + 1, rows), :],
                below,
                above,
            )

        coeff_names = ("xm", "xp", "ym", "yp", "zm", "zp")

        def applied(lv, buf, lo, rows, halo):
            mid, near = around(lv, buf, lo, rows, halo)
            span = pl.ds(lo, rows)
            total = mid
            for name, value in zip(coeff_names, near):
                total = total - ref[lv.index, name][span, :] * value
            return mid, total

        def prepare(lv, buf, halo):
            keep = ref[lv.index, "k"]
            keep[...] = jnp.ones((lv.n, LANES), jnp.float32)
            keep[pl.ds(0, lv.nx, stride=lv.pitch), :] = jnp.zeros((lv.nx, LANES), jnp.float32)
            keep[pl.ds(lv.pitch - 1, lv.nx, stride=lv.pitch), :] = jnp.zeros((lv.nx, LANES), jnp.float32)
            for lo, rows in lv.groups():
                span = pl.ds(lo, rows)
                mid, near = around(lv, buf, lo, rows, halo)
                where = iota((rows, LANES), 1)
                near = list(near)
                if lv.shared and lv.nz == LANES:
                    near[4] = jnp.where(where == 0, 0.0, near[4])
                    near[5] = jnp.where(where == LANES - 1, 0.0, near[5])
                inside = keep[span, :] > 0.5
                if lv.nz < LANES:
                    inside = inside & (where >= lv.zo) & (where < lv.nz + lv.zo)
                couple = [(0.5 * lv.factor) * (mid + value) for value in near]
                diagonal = couple[0]
                for value in couple[1:]:
                    diagonal = diagonal + value
                inverse = jnp.where(inside, 1.0 / diagonal, 0.0)
                ref[lv.index, "dg"][span, :] = diagonal
                ref[lv.index, "iv"][span, :] = inverse
                couple = [value * inverse for value in couple]
                if lv.shared and lv.nz == LANES:
                    couple[4] = jnp.where(where == 0, 0.0, couple[4])
                    couple[5] = jnp.where(where == LANES - 1, 0.0, couple[5])
                for name, value in zip(coeff_names, couple):
                    ref[lv.index, name][span, :] = value

        def sweeps(lv, src, first, count, final, lift):
            factors = chebyshev_factors(count)
            r, u = ref[lv.index, "r"], ref[lv.index, "u"]
            buffers = [ref[lv.index, "d0"], ref[lv.index, "d1"]]
            held = src
            for step in range(count):
                keep, push = factors[step]
                target = buffers[step % 2]
                halo = faces(lv, held) if held is not None else None
                for lo, rows in lv.groups():
                    span = pl.ds(lo, rows)
                    value = r[span, :]
                    if held is not None:
                        mid, change = applied(lv, held, lo, rows, halo)
                        value = value - change
                        r[span, :] = value
                    direction = push * value
                    if step > 0:
                        direction = direction + keep * mid
                    target[pl.ds(lv.c0 + lo, rows), :] = direction
                    if step == 0 and src is None:
                        u[span, :] = direction
                    elif step == 0:
                        u[span, :] = u[span, :] + mid + direction
                    else:
                        u[span, :] = u[span, :] + direction
                held = target
            if final:
                halo = faces(lv, held)
                for lo, rows in lv.groups():
                    span = pl.ds(lo, rows)
                    mid, change = applied(lv, held, lo, rows, halo)
                    r[span, :] = r[span, :] - change
            return held

        def halve(lv, buf, base):
            out = ref[None, "half"]
            nx, ny = lv.nx // 2, lv.ny // 2
            for x in range(nx):
                total = None
                for px in range(2):
                    for py in range(2):
                        at = base + (2 * x + px) * lv.pitch + 1 + py
                        value = buf[pl.ds(at, ny, stride=2), :]
                        total = value if total is None else total + value
                out[pl.ds(x * ny, ny), :] = total
            return nx, ny

        def pair_matrix(lv, offset):
            fine, coarse = iota((LANES, LANES), 0), iota((LANES, LANES), 1)
            cell = fine - lv.zo
            inside = (cell >= 0) & (cell < lv.nz)
            match = lax.shift_right_arithmetic(cell, 1) + offset == coarse
            return jnp.where(inside & match, 0.125, 0.0)

        def restrict(lv, buf, base, offset):
            nx, ny = halve(lv, buf, base)
            return nx, ny, dot(ref[None, "half"][pl.ds(0, up8(nx * ny)), :], pair_matrix(lv, offset))

        def spread(nx, ny, value, coarse, buf, base):
            scratch_ref = ref[None, "half"]
            scratch_ref[pl.ds(0, up8(nx * ny)), :] = value
            for x in range(nx):
                buf[pl.ds(base + x * coarse.pitch + 1, ny), :] = scratch_ref[pl.ds(x * ny, ny), :]

        def stretch(cell, offset):
            coarse = iota((LANES, LANES), 0) - offset
            parent = lax.shift_right_arithmetic(cell, 1)
            other = parent + 2 * (cell & 1) - 1
            return jnp.where(coarse == parent, 0.75, 0.0) + jnp.where(coarse == other, 0.25, 0.0)

        def prolong(rows, pitch, c0, nx, ny, weights, value, fine, buf):
            t, te, to = ref[None, "t"], ref[None, "te"], ref[None, "to"]
            t[pl.ds(0, rows), :] = dot(value, weights)
            n = nx * pitch
            mid = t[pl.ds(c0, n), :]
            te[pl.ds(0, n), :] = 0.75 * mid + 0.25 * t[pl.ds(c0 - pitch, n), :]
            to[pl.ds(0, n), :] = 0.75 * mid + 0.25 * t[pl.ds(c0 + pitch, n), :]
            for x in range(nx):
                for px, src in ((0, te), (1, to)):
                    at = x * pitch + 1
                    mid = 0.75 * src[pl.ds(at, ny), :]
                    to_row = fine.c0 + (2 * x + px) * fine.pitch + 1
                    buf[pl.ds(to_row, ny, stride=2), :] = mid + 0.25 * src[pl.ds(at - 1, ny), :]
                    buf[pl.ds(to_row + 1, ny, stride=2), :] = mid + 0.25 * src[pl.ds(at + 1, ny), :]

        def columns(fine):
            return iota((LANES, LANES), 1) - fine.zo

        def masked(fine, weights):
            cell = columns(fine)
            return jnp.where((cell >= 0) & (cell < fine.nz), weights, 0.0)

        def depth_copy(which, k):
            return pltpu.make_async_remote_copy(
                src_ref=ref[None, "zs"].at[which],
                dst_ref=ref[None, "zr"].at[which, gz],
                send_sem=ref[None, "zsend"].at[which, k],
                recv_sem=ref[None, "zrecv"].at[which, k],
                device_id=(gx, gy, depth_peer(k)),
                device_id_type=MESH,
            )

        def depth_arrival(which, k):
            source = lax.rem(gz + gzn - k, gzn)
            return pltpu.make_async_remote_copy(
                src_ref=ref[None, "zs"].at[which],
                dst_ref=ref[None, "zr"].at[which, source],
                send_sem=ref[None, "zsend"].at[which, k],
                recv_sem=ref[None, "zrecv"].at[which, k],
                device_id=(gx, gy, depth_peer(k)),
                device_id_type=MESH,
            )

        def plane_copy(which, i, j):
            px, py = plane_peer(i, j)
            return pltpu.make_async_remote_copy(
                src_ref=ref[None, "ps"].at[which],
                dst_ref=ref[None, "pr"].at[which, gx * gyn + gy],
                send_sem=ref[None, "psend"].at[which, i * gyn + j],
                recv_sem=ref[None, "precv"].at[which, i * gyn + j],
                device_id=(px, py, gz),
                device_id_type=MESH,
            )

        def plane_arrival(which, i, j):
            sx, sy = lax.rem(gx + gxn - i, gxn), lax.rem(gy + gyn - j, gyn)
            px, py = plane_peer(i, j)
            return pltpu.make_async_remote_copy(
                src_ref=ref[None, "ps"].at[which],
                dst_ref=ref[None, "pr"].at[which, sx * gyn + sy],
                send_sem=ref[None, "psend"].at[which, i * gyn + j],
                recv_sem=ref[None, "precv"].at[which, i * gyn + j],
                device_id=(px, py, gz),
                device_id_type=MESH,
            )

        def gather_depth_start(which, block):
            ref[None, "zs"][which] = block[:blk]
            for k in range(1, gzn):
                depth_copy(which, k).start()

        def gather_plane_start(which):
            total = ref[None, "zs"][which]
            for k in range(1, gzn):
                depth_arrival(which, k).wait_recv()
            for k in range(1, gzn):
                total = total + ref[None, "zr"][which, lax.rem(gz + k, gzn)]
            ref[None, "ps"][which] = total
            for i, j in plane_peers:
                plane_copy(which, i, j).start()
            ref[None, "pr"][which, gx * gyn + gy] = total

        def gather_end(which, buf, base):
            for i, j in plane_peers:
                plane_arrival(which, i, j).wait_recv()
            for i in range(gxn):
                for x in range(cx):
                    for y in range(cy):
                        rows = [ref[None, "pr"][which, i * gyn + j, pl.ds(x * cy + y, 1), :] for j in range(gyn)]
                        at = base + (i * cx + x) * three.pitch + 1 + y
                        buf[pl.ds(at, gyn, stride=cy), :] = jnp.concatenate(rows, axis=0)

        def gather_waits():
            for which in range(2):
                for k in range(1, gzn):
                    depth_copy(which, k).wait_send()
                for i, j in plane_peers:
                    plane_copy(which, i, j).wait_send()

        first = local[0]
        for x in range(first.nx):
            ref[0, "v"][pl.ds(first.c0 + x * first.pitch + 1, first.ny), :] = k_ref[x]
        for index in range(2):
            fine, coarse = local[index], local[index + 1]
            nx, ny, value = restrict(fine, ref[index, "v"], fine.c0, coarse.zo)
            spread(nx, ny, value, coarse, ref[index + 1, "v"], coarse.c0)
        last = local[2]
        _, _, k_block = restrict(last, ref[2, "v"], last.c0, gz * cz + three.zo)

        pl.semaphore_wait(barrier, len(plane_peers) + gzn - 1)

        slots = [begin_faces(lv, ref[lv.index, "v"]) for lv in local]
        gather_depth_start(0, k_block)
        for x in range(first.nx):
            ref[0, "r"][pl.ds(x * first.pitch + 1, first.ny), :] = b_ref[x]
        halo = end_faces(local[0], ref[0, "v"], slots[0])
        prepare(local[0], ref[0, "v"], halo)
        for lv in local[1:]:
            end_faces(lv, ref[lv.index, "v"], slots[lv.index])
            prepare(lv, ref[lv.index, "v"], None)
        gather_plane_start(0)

        zero_edge = jnp.zeros((first.nx, LANES), jnp.float32)
        for at in (0, first.pitch - 1):
            ref[0, "r"][pl.ds(at, first.nx, stride=first.pitch), :] = zero_edge
        for lv in local:
            r, dg, iv = (ref[lv.index, name] for name in ("r", "dg", "iv"))
            r[...] = r[...] * iv[...]
            sweeps(lv, None, True, STEPS, True, False)
            residual = ref[lv.index, "v"]
            residual[pl.ds(lv.c0, lv.n), :] = r[...] * dg[...]
            if lv.index < 2:
                coarse = local[lv.index + 1]
                nx, ny, value = restrict(lv, residual, lv.c0, coarse.zo)
                ref[coarse.index, "r"][...] = jnp.zeros((coarse.n, LANES), jnp.float32)
                spread(nx, ny, value, coarse, ref[coarse.index, "r"], 0)
        _, _, b_block = restrict(last, ref[2, "v"], last.c0, gz * cz + three.zo)
        gather_depth_start(1, b_block)
        gather_end(0, ref[3, "v"], three.c0)
        prepare(three, ref[3, "v"], None)
        nx, ny, value = restrict(three, ref[3, "v"], three.c0, four.zo)
        spread(nx, ny, value, four, ref[4, "v"], four.c0)
        prepare(four, ref[4, "v"], None)
        ref[3, "r"][...] = jnp.zeros((three.n, LANES), jnp.float32)
        ref[4, "r"][...] = jnp.zeros((four.n, LANES), jnp.float32)
        gather_plane_start(1)
        gather_end(1, ref[3, "r"], 0)

        r3, r4 = ref[3, "r"], ref[4, "r"]
        r3[...] = r3[...] * ref[3, "iv"][...]
        sweeps(three, None, True, STEPS, True, False)
        ref[3, "v"][pl.ds(three.c0, three.n), :] = r3[...] * ref[3, "dg"][...]
        nx, ny, value = restrict(three, ref[3, "v"], three.c0, four.zo)
        spread(nx, ny, value, four, r4, 0)
        r4[...] = r4[...] * ref[4, "iv"][...]
        sweeps(four, None, True, COARSE_STEPS, False, False)

        ref[4, "v"][pl.ds(four.c0, four.n), :] = ref[4, "u"][...]
        prolong(
            four.rows, four.pitch, four.c0, four.nx, four.ny,
            masked(three, stretch(columns(three), four.zo)), ref[4, "v"][...], three, ref[3, "v"],
        )
        for at in (0, three.pitch - 1):
            ref[3, "v"][pl.ds(three.c0 + at, three.nx, stride=three.pitch), :] = jnp.zeros(
                (three.nx, LANES), jnp.float32
            )
        sweeps(three, ref[3, "v"], True, STEPS, False, False)
        ref[3, "v"][pl.ds(three.c0, three.n), :] = ref[3, "u"][...]

        pitch = cy + 2
        picked = up8((cx + 2) * pitch)
        row, source = iota((picked, three.rows), 0), iota((picked, three.rows), 1)
        box_x = row // pitch
        wanted = three.c0 + (gx * cx - 1 + box_x) * three.pitch + gy * cy + (row - box_x * pitch)
        window = dot(jnp.where(source == wanted, 1.0, 0.0), ref[3, "v"][...])
        weights = stretch(columns(last) + gz * last.nz, three.zo)
        prolong(picked, pitch, pitch, cx, cy, masked(last, weights), window, last, ref[2, "v"])
        for lv in reversed(local):
            sweeps(lv, ref[lv.index, "v"], True, STEPS, lv.index == 0, False)
            if lv.index:
                field = ref[lv.index, "v"]
                field[pl.ds(lv.c0, lv.n), :] = ref[lv.index, "u"][...]
                corners(lv, field)
                fine = local[lv.index - 1]
                weights = masked(fine, stretch(columns(fine), lv.zo))
                prolong(lv.rows, lv.pitch, lv.c0, lv.nx, lv.ny, weights, field[...], fine, ref[fine.index, "v"])

        for x in range(first.nx):
            span = pl.ds(x * first.pitch + 1, first.ny)
            u_ref[x] = ref[0, "u"][span, :]
            res_ref[x] = ref[0, "r"][span, :] * ref[0, "dg"][span, :]

        for lv in local:
            for slot in range(counters[lv.index]):
                for way in range(6):

                    @pl.when(has[way])
                    def _():
                        link(lv, slot, way).wait_send()

        gather_waits()

    def on_device(right_side, conductivity):
        out = jax.ShapeDtypeStruct(box, jnp.float32)
        return pl.pallas_call(
            kernel,
            out_shape=(out, out),
            in_specs=[pl.BlockSpec(memory_space=pltpu.VMEM)] * 2,
            out_specs=[pl.BlockSpec(memory_space=pltpu.VMEM)] * 2,
            scratch_shapes=shapes,
            compiler_params=pltpu.CompilerParams(
                collective_id=0, has_side_effects=True, vmem_limit_bytes=48 * 1024 * 1024
            ),
        )(right_side, conductivity)

    return on_device


def solution(mesh):
    sizes = tuple(mesh.shape[axis] for axis in ("gx", "gy", "gz"))
    spec = P("gx", "gy", "gz")
    return jax.shard_map(
        build(sizes, (32, 16, 128)), mesh=mesh, in_specs=(spec, spec), out_specs=(spec, spec), check_vma=False
    )
```

profile of v0, /device:TPU:1, one launch (start us, length us, event | category | flops | bytes accessed | tf_op | source)
XLA Modules:
  0.0 116.2 jit_solution(5813177669547939400)
XLA Ops:
  0.6 0.0 copy-start
  0.6 0.9 copy-done
  1.6 0.0 copy-start.1
  1.6 0.9 copy-done.1
  2.5 112.2 %shard_map.41 = (f32[32,16,128]{2,1,0:T(8,128)S(1)}, f32[32,16,128]{2,1,0:T(8,128)S(1)}) custom-call(f32[32,16,128]{2,1,0:T(8,128)S(1)} %copy-done, f32[32,16,128]{2,1,0:T(8,128)S(1)} %copy-done.1), custom_call_target="tpu_custom_call" | custom-call | tf_op jit(solution)/shard_map/pallas_call | solution.py:630
  114.7 0.7 copy.6
  115.5 0.7 copy.7
Async XLA Ops:
  0.6 1.0 copy-start
  1.6 0.9 copy-start.1
where the time goes:
time: 116 us
  Pallas kernels  112 us (97%)
  local copies, waits for them, and re-layouts  3.3 us (3%)
    pallas_call x1, Pallas kernels, on_device(): pl.pallas_call(kernel, out_shape=(out, out), in_specs=[pl.BlockSpec(memor...  112 us
    unnamed x6, local copies, waits for them, and re-layouts  3.3 us

commit v1 on v0

v1 whole, which is shorter than its diff:
```python
import jax
import jax.numpy as jnp
from jax import lax
from jax.experimental import pallas as pl
from jax.experimental.pallas import tpu as pltpu
from jax.sharding import PartitionSpec as P

STEPS = 3
COARSE_STEPS = 8
LOWER_EDGE = 0.3
UPPER_EDGE = 2.0
MESH = pl.DeviceIdType.MESH
LANES = 128
EXCHANGES = 8
DEEP = 4
HALO = 4
OFFSETS = [(i, j, k) for i in (-1, 0, 1) for j in (-1, 0, 1) for k in (-1, 0, 1) if i or j or k]
EDGES = [offset for offset in OFFSETS if offset[2]]


def chebyshev_factors(sweeps):
    centre_value = 0.5 * (UPPER_EDGE + LOWER_EDGE)
    half_width = 0.5 * (UPPER_EDGE - LOWER_EDGE)
    ratio_value = centre_value / half_width
    damping = 1.0 / ratio_value
    factors = [(0.0, 1.0 / centre_value)]
    for _ in range(1, sweeps):
        damping_next = 1.0 / (2.0 * ratio_value - damping)
        factors.append((damping_next * damping, 2.0 * damping_next / half_width))
        damping = damping_next
    return factors


def up8(value):
    return -(-value // 8) * 8


class Level:
    def __init__(self, index, nx, ny, nz, h, shared):
        self.index, self.nx, self.ny, self.nz, self.h, self.shared = index, nx, ny, nz, h, shared
        self.pitch = ny + 2 * h
        self.c0 = up8(self.pitch + 1)
        self.n = up8((nx + 2 * h - 2) * self.pitch)
        self.rows = self.c0 + self.n + up8(self.pitch + 1)
        self.zo = 0 if nz == LANES else h
        self.factor = 0.25**index
        self.wide = nz == LANES and not shared
        self.deep = h > 1
        self.chunks = self.n // 8
        self.half = -(-self.chunks // 2)

    def row(self, x, y):
        return self.c0 + (x + self.h - 1) * self.pitch + y + self.h

    def scratch(self):
        field = pltpu.VMEM((self.n, LANES), jnp.float32)
        padded = pltpu.VMEM((self.rows, LANES), jnp.float32)
        shapes = {name: field for name in ("xm", "xp", "ym", "yp", "zm", "zp", "dg", "iv", "r", "u")}
        shapes.update({name: padded for name in ("d0", "d1", "v", "w")})
        count = EXCHANGES
        if self.deep:
            for name in ("s", "q"):
                shapes[name + "x"] = pltpu.VMEM((DEEP, 2, self.h * self.ny, LANES), jnp.float32)
                shapes[name + "y"] = pltpu.VMEM((DEEP, 2, self.h * self.nx, LANES), jnp.float32)
                shapes[name + "c"] = pltpu.VMEM((DEEP, 4, self.h * self.h, LANES), jnp.float32)
            shapes["sz"] = pltpu.VMEM((DEEP, 8, LANES), jnp.float32)
            shapes["qz"] = pltpu.VMEM((DEEP, 18, 8, LANES), jnp.float32)
            shapes["zone"] = pltpu.VMEM((6, up8(self.pitch), LANES), jnp.float32)
            shapes["send"] = pltpu.SemaphoreType.DMA((DEEP, 26))
            shapes["recv"] = pltpu.SemaphoreType.DMA((DEEP, 26))
        elif not self.shared:
            for name in ("s", "q"):
                shapes[name + "x"] = pltpu.VMEM((count, 2, self.ny, LANES), jnp.float32)
                shapes[name + "y"] = pltpu.VMEM((count, 2, self.nx, LANES), jnp.float32)
            shapes["sz"] = pltpu.VMEM((count, 16, LANES), jnp.float32)
            shapes["qz"] = pltpu.VMEM((count, 2, 16, LANES), jnp.float32)
            shapes["send"] = pltpu.SemaphoreType.DMA((count, 6))
            shapes["recv"] = pltpu.SemaphoreType.DMA((count, 6))
        return shapes

    def groups(self):
        count = -(-self.n // 96)
        size = up8(-(-self.n // count))
        return [(lo, min(size, self.n - lo)) for lo in range(0, self.n, size)]


def dot(a, b):
    return jnp.dot(a, b, precision=lax.Precision.HIGHEST, preferred_element_type=jnp.float32)


def iota(shape, dim):
    return lax.broadcasted_iota(jnp.int32, shape, dim)


def roll(value, shift):
    shift %= LANES
    return pltpu.roll(value, shift, 1) if shift else value


def build(mesh_shape, box):
    gxn, gyn, gzn = mesh_shape
    bx, by, bz = box
    local = [Level(i, bx >> i, by >> i, bz >> i, HALO if i else 1, False) for i in range(3)]
    cx, cy, cz = bx >> 3, by >> 3, bz >> 3
    three = Level(3, gxn * cx, gyn * cy, gzn * cz, 1, True)
    four = Level(4, three.nx // 2, three.ny // 2, three.nz // 2, 1, True)
    levels = local + [three, four]
    blk = cx * cy
    names = [(lv.index, name) for lv in levels for name in lv.scratch()]
    shapes = [shape for lv in levels for shape in lv.scratch().values()]
    extra = {
        "t": pltpu.VMEM((max(lv.rows for lv in levels), LANES), jnp.float32),
        "te": pltpu.VMEM((max(lv.n for lv in levels) + 16, LANES), jnp.float32),
        "to": pltpu.VMEM((max(lv.n for lv in levels) + 16, LANES), jnp.float32),
        "half": pltpu.VMEM((128, LANES), jnp.float32),
        "zs": pltpu.VMEM((2, blk, LANES), jnp.float32),
        "zr": pltpu.VMEM((2, gzn, blk, LANES), jnp.float32),
        "ps": pltpu.VMEM((2, blk, LANES), jnp.float32),
        "pr": pltpu.VMEM((2, gxn * gyn, blk, LANES), jnp.float32),
        "zsend": pltpu.SemaphoreType.DMA((2, gzn)),
        "zrecv": pltpu.SemaphoreType.DMA((2, gzn)),
        "psend": pltpu.SemaphoreType.DMA((2, gxn * gyn)),
        "precv": pltpu.SemaphoreType.DMA((2, gxn * gyn)),
    }
    names += [(None, name) for name in extra]
    shapes += list(extra.values())

    def kernel(b_ref, k_ref, u_ref, res_ref, *scratch):
        ref = {key: value for key, value in zip(names, scratch)}
        gx, gy, gz = lax.axis_index("gx"), lax.axis_index("gy"), lax.axis_index("gz")
        has = (gx > 0, gx < gxn - 1, gy > 0, gy < gyn - 1, gz > 0, gz < gzn - 1)
        peer = (
            (gx - 1, gy, gz),
            (gx + 1, gy, gz),
            (gx, gy - 1, gz),
            (gx, gy + 1, gz),
            (gx, gy, gz - 1),
            (gx, gy, gz + 1),
        )
        lane = iota((8, LANES), 1)
        plane_peers = [(i, j) for i in range(gxn) for j in range(gyn) if i or j]

        def plane_peer(i, j):
            return lax.rem(gx + i, gxn), lax.rem(gy + j, gyn)

        def depth_peer(k):
            return lax.rem(gz + k, gzn)

        for lv in levels:
            for name in ("d0", "d1", "v", "w"):
                ref[lv.index, name][...] = jnp.zeros((lv.rows, LANES), jnp.float32)
            if not lv.shared:
                for name in ("qx", "qy", "qz") + (("qc",) if lv.deep else ()):
                    target = ref[lv.index, name]
                    target[...] = jnp.zeros(target.shape, jnp.float32)

        barrier = pltpu.get_barrier_semaphore()
        for i, j in plane_peers:
            px, py = plane_peer(i, j)
            pl.semaphore_signal(barrier, inc=1, device_id=(px, py, gz), device_id_type=MESH)
        for k in range(1, gzn):
            pl.semaphore_signal(barrier, inc=1, device_id=(gx, gy, depth_peer(k)), device_id_type=MESH)

        counters = [0, 0, 0]
        at = (gx, gy, gz)
        sizes = (gxn, gyn, gzn)

        def there(offset):
            found = jnp.bool_(True)
            for a in range(3):
                if offset[a] < 0:
                    found = found & (at[a] > 0)
                elif offset[a] > 0:
                    found = found & (at[a] < sizes[a] - 1)
            return found

        exists = {offset: there(offset) for offset in OFFSETS}

        def device(offset):
            return tuple(at[a] + offset[a] for a in range(3))

        diagonal = [offset for offset in EDGES if offset[0] or offset[1]]
        for offset in diagonal:
            around_edge = tuple(lax.rem(at[a] + offset[a] + sizes[a], sizes[a]) for a in range(3))
            pl.semaphore_signal(barrier, inc=1, device_id=around_edge, device_id_type=MESH)

        def link(lv, slot, way):
            axis, side = "xyz"[way // 2], way % 2
            source = ref[lv.index, "s" + axis].at[slot]
            if axis != "z":
                source = source.at[side]
            return pltpu.make_async_remote_copy(
                src_ref=source,
                dst_ref=ref[lv.index, "q" + axis].at[slot, 1 - side],
                send_sem=ref[lv.index, "send"].at[slot, way],
                recv_sem=ref[lv.index, "recv"].at[slot, way ^ 1],
                device_id=peer[way],
                device_id_type=MESH,
            )

        def incoming(lv, slot, way):
            axis, side = "xyz"[way // 2], way % 2
            source = ref[lv.index, "s" + axis].at[slot]
            if axis != "z":
                source = source.at[side]
            return pltpu.make_async_remote_copy(
                src_ref=source,
                dst_ref=ref[lv.index, "q" + axis].at[slot, side],
                send_sem=ref[lv.index, "send"].at[slot, way],
                recv_sem=ref[lv.index, "recv"].at[slot, way],
                device_id=peer[way],
                device_id_type=MESH,
            )

        def start(lv, slot, ways):
            for way in ways:

                @pl.when(has[way])
                def _():
                    link(lv, slot, way).start()

        def finish(lv, slot, ways):
            for way in ways:

                @pl.when(has[way])
                def _():
                    incoming(lv, slot, way).wait_recv()

        def begin_faces(lv, buf):
            slot = counters[lv.index]
            counters[lv.index] += 1
            out = ref[lv.index, "sx"]
            out[slot, 0] = buf[pl.ds(lv.row(0, 0), lv.ny), :]
            out[slot, 1] = buf[pl.ds(lv.row(lv.nx - 1, 0), lv.ny), :]
            start(lv, slot, (0, 1))
            out = ref[lv.index, "sy"]
            out[slot, 0] = buf[pl.ds(lv.row(0, 0), lv.nx, stride=lv.pitch), :]
            out[slot, 1] = buf[pl.ds(lv.row(0, lv.ny - 1), lv.nx, stride=lv.pitch), :]
            start(lv, slot, (2, 3))
            out = ref[lv.index, "sz"]
            packed = jnp.zeros((8, LANES), jnp.float32)
            for c in range(lv.chunks):
                cc = c % lv.half
                value = buf[pl.ds(lv.c0 + 8 * c, 8), :]
                packed = jnp.where(lane >= 2 * cc, roll(value, 2 * cc + 1), packed)
                if cc == lv.half - 1 or c == lv.chunks - 1:
                    out[slot, pl.ds(8 * (c // lv.half), 8), :] = packed
            start(lv, slot, (4, 5))
            return slot

        def end_faces(lv, buf, slot):
            finish(lv, slot, range(6))
            got = ref[lv.index, "qx"]
            buf[pl.ds(lv.row(-1, 0), lv.ny), :] = got[slot, 0]
            buf[pl.ds(lv.row(lv.nx, 0), lv.ny), :] = got[slot, 1]
            got = ref[lv.index, "qy"]
            buf[pl.ds(lv.row(0, -1), lv.nx, stride=lv.pitch), :] = got[slot, 0]
            buf[pl.ds(lv.row(0, lv.ny), lv.nx, stride=lv.pitch), :] = got[slot, 1]
            got = ref[lv.index, "qz"]
            even = lane % 2 == 0
            return [
                jnp.where(even, got[slot, 0, pl.ds(8 * h, 8), :], roll(got[slot, 1, pl.ds(8 * h, 8), :], -2))
                for h in range(2)
            ]

        def faces(lv, buf):
            return end_faces(lv, buf, begin_faces(lv, buf)) if lv.wide else None

        def deep_link(lv, slot, offset, arriving):
            i, j, k = offset
            sent = OFFSETS.index(offset)
            landed = sent if arriving else OFFSETS.index((-i, -j, -k))

            def part(kind, which):
                if k:
                    return ref[lv.index, kind + "z"].at[(slot,) if which is None else (slot, which)]
                name = "c" if i and j else "x" if i else "y"
                return ref[lv.index, kind + name].at[slot, which]

            def place(offset):
                if offset[2]:
                    return EDGES.index(offset)
                low_x, low_y = offset[0] > 0, offset[1] > 0
                return 2 * low_x + low_y if offset[0] and offset[1] else int(low_x or low_y)

            return pltpu.make_async_remote_copy(
                src_ref=part("s", None if k else place(offset)),
                dst_ref=part("q", place(OFFSETS[landed])),
                send_sem=ref[lv.index, "send"].at[slot, sent],
                recv_sem=ref[lv.index, "recv"].at[slot, landed],
                device_id=device(offset),
                device_id_type=MESH,
            )

        def deep_start(lv, slot, offsets):
            for offset in offsets:

                @pl.when(exists[offset])
                def _():
                    deep_link(lv, slot, offset, False).start()

        def deep_finish(lv, slot, offsets):
            for offset in offsets:

                @pl.when(exists[offset])
                def _():
                    deep_link(lv, slot, offset, True).wait_recv()

        def near_side(size, direction, h):
            return 0 if direction < 0 else size - h

        def far_side(size, direction, h):
            return -h if direction < 0 else size

        def begin_deep(lv, buf):
            slot = counters[lv.index]
            counters[lv.index] += 1
            h, nx, ny, nz = lv.h, lv.nx, lv.ny, lv.nz
            out = ref[lv.index, "sz"]
            packed = jnp.zeros((ny, LANES), jnp.float32)
            where = iota((ny, LANES), 1)
            for x in range(nx):
                value = buf[pl.ds(lv.row(x, 0), ny), :]
                low = 2 * h * x
                packed = jnp.where(where >= low, roll(value, low - h), packed)
                packed = jnp.where(where >= low + h, roll(value, low + h - nz), packed)
            out[slot, pl.ds(0, ny), :] = packed
            if ny < 8:
                out[slot, pl.ds(ny, 8 - ny), :] = packed[: 8 - ny]
            deep_start(lv, slot, EDGES)
            for side in (-1, 1):
                x0, y0 = near_side(nx, side, h), near_side(ny, side, h)
                for p in range(h):
                    ref[lv.index, "sx"][slot, int(side > 0), pl.ds(p * ny, ny), :] = buf[pl.ds(lv.row(x0 + p, 0), ny), :]
                    ref[lv.index, "sy"][slot, int(side > 0), pl.ds(p * nx, nx), :] = buf[
                        pl.ds(lv.row(0, y0 + p), nx, stride=lv.pitch), :
                    ]
            for i in (-1, 1):
                for j in (-1, 1):
                    x0, y0 = near_side(nx, i, h), near_side(ny, j, h)
                    for p in range(h):
                        ref[lv.index, "sc"][slot, 2 * (i > 0) + (j > 0), pl.ds(p * h, h), :] = buf[
                            pl.ds(lv.row(x0 + p, y0), h), :
                        ]
            deep_start(lv, slot, [offset for offset in OFFSETS if not offset[2]])
            return slot

        def end_deep(lv, buf, slot):
            h, nx, ny, nz = lv.h, lv.nx, lv.ny, lv.nz
            deep_finish(lv, slot, [offset for offset in OFFSETS if not offset[2]])
            for side in (-1, 1):
                x0, y0 = far_side(nx, side, h), far_side(ny, side, h)
                for p in range(h):
                    buf[pl.ds(lv.row(x0 + p, 0), ny), :] = ref[lv.index, "qx"][slot, int(side > 0), pl.ds(p * ny, ny), :]
                    buf[pl.ds(lv.row(0, y0 + p), nx, stride=lv.pitch), :] = ref[lv.index, "qy"][
                        slot, int(side > 0), pl.ds(p * nx, nx), :
                    ]
            for i in (-1, 1):
                for j in (-1, 1):
                    x0, y0 = far_side(nx, i, h), far_side(ny, j, h)
                    for p in range(h):
                        buf[pl.ds(lv.row(x0 + p, y0), h), :] = ref[lv.index, "qc"][
                            slot, 2 * (i > 0) + (j > 0), pl.ds(p * h, h), :
                        ]
            deep_finish(lv, slot, EDGES)
            got, zone = ref[lv.index, "qz"], ref[lv.index, "zone"]
            for i in (-1, 0, 1):
                for k in (-1, 1):
                    place = 2 * (i + 1) + (k > 0)
                    zone[place, pl.ds(0, h), :] = got[slot, EDGES.index((i, -1, k)), pl.ds(ny - h, h), :]
                    middle = (i, 0, k)
                    zone[place, pl.ds(h, ny), :] = got[slot, EDGES.index(middle), pl.ds(0, ny), :]
                    zone[place, pl.ds(h + ny, h), :] = got[slot, EDGES.index((i, 1, k)), pl.ds(0, h), :]
            where = iota((lv.pitch, LANES), 1)
            edge = (where < h) | ((where >= nz + h) & (where < nz + 2 * h))
            high = (where & (2 * h - 1)) >= h
            for i in (-1, 0, 1):
                low, up = (zone[2 * (i + 1) + k, pl.ds(0, lv.pitch), :] for k in (0, 1))
                merged = jnp.where(high, low, roll(up, nz + 2 * h))
                planes = range(nx) if i == 0 else range(-h, 0) if i < 0 else range(nx, nx + h)
                for x in planes:
                    span = pl.ds(lv.row(x, -h), lv.pitch)
                    buf[span, :] = jnp.where(edge, roll(merged, -(2 * h * (x - i * nx) + h)), buf[span, :])

        def sides(lv, mid, lo, rows, halo):
            below, above = roll(mid, 1), roll(mid, -1)
            if lv.wide:
                edge = jnp.concatenate(
                    [
                        roll(halo[c // lv.half], -2 * (c % lv.half))
                        for c in range(lo // 8, (lo + rows) // 8)
                    ],
                    axis=0,
                )
                where = iota((rows, LANES), 1)
                below = jnp.where(where == 0, edge, below)
                above = jnp.where(where == LANES - 1, edge, above)
            return below, above

        def around(lv, buf, lo, rows, halo):
            base = lv.c0 + lo
            mid = buf[pl.ds(base, rows), :]
            below, above = sides(lv, mid, lo, rows, halo)
            return mid, (
                buf[pl.ds(base - lv.pitch, rows), :],
                buf[pl.ds(base + lv.pitch, rows), :],
                buf[pl.ds(base - 1, rows), :],
                buf[pl.ds(base + 1, rows), :],
                below,
                above,
            )

        coeff_names = ("xm", "xp", "ym", "yp", "zm", "zp")

        def applied(lv, buf, lo, rows, halo):
            mid, near = around(lv, buf, lo, rows, halo)
            span = pl.ds(lo, rows)
            total = mid
            for name, value in zip(coeff_names, near):
                total = total - ref[lv.index, name][span, :] * value
            return mid, total

        def prepare(lv, buf, halo):
            for lo, rows in lv.groups():
                span = pl.ds(lo, rows)
                mid, near = around(lv, buf, lo, rows, halo)
                where = iota((rows, LANES), 1)
                near = list(near)
                if lv.shared and lv.nz == LANES:
                    near[4] = jnp.where(where == 0, 0.0, near[4])
                    near[5] = jnp.where(where == LANES - 1, 0.0, near[5])
                couple = [(0.5 * lv.factor) * (mid + value) for value in near]
                diagonal = couple[0]
                for value in couple[1:]:
                    diagonal = diagonal + value
                inverse = jnp.where(mid > 0.0, 1.0 / diagonal, 0.0)
                ref[lv.index, "dg"][span, :] = diagonal
                ref[lv.index, "iv"][span, :] = inverse
                couple = [value * inverse for value in couple]
                if lv.shared and lv.nz == LANES:
                    couple[4] = jnp.where(where == 0, 0.0, couple[4])
                    couple[5] = jnp.where(where == LANES - 1, 0.0, couple[5])
                for name, value in zip(coeff_names, couple):
                    ref[lv.index, name][span, :] = value

        def sweeps(lv, src, count, final):
            factors = chebyshev_factors(count)
            r, u = ref[lv.index, "r"], ref[lv.index, "u"]
            buffers = [ref[lv.index, "d0"], ref[lv.index, "d1"]]
            held = src
            for step in range(count):
                keep, push = factors[step]
                target = buffers[step % 2]
                halo = faces(lv, held) if held is not None else None
                for lo, rows in lv.groups():
                    span = pl.ds(lo, rows)
                    value = r[span, :]
                    if held is not None:
                        mid, change = applied(lv, held, lo, rows, halo)
                        value = value - change
                        r[span, :] = value
                    direction = push * value
                    if step > 0:
                        direction = direction + keep * mid
                    target[pl.ds(lv.c0 + lo, rows), :] = direction
                    if step == 0 and src is None:
                        u[span, :] = direction
                    elif step == 0:
                        u[span, :] = u[span, :] + mid + direction
                    else:
                        u[span, :] = u[span, :] + direction
                held = target
            if final:
                halo = faces(lv, held)
                for lo, rows in lv.groups():
                    span = pl.ds(lo, rows)
                    mid, change = applied(lv, held, lo, rows, halo)
                    r[span, :] = r[span, :] - change
            return held

        def halve(lv, buf):
            out = ref[None, "half"]
            nx, ny = lv.nx // 2, lv.ny // 2
            for x in range(nx):
                total = None
                for px in range(2):
                    for py in range(2):
                        at = lv.row(2 * x + px, py)
                        value = buf[pl.ds(at, ny, stride=2), :]
                        total = value if total is None else total + value
                out[pl.ds(x * ny, ny), :] = total
            return nx, ny

        def pair_matrix(lv, offset):
            fine, coarse = iota((LANES, LANES), 0), iota((LANES, LANES), 1)
            cell = fine - lv.zo
            inside = (cell >= 0) & (cell < lv.nz)
            match = lax.shift_right_arithmetic(cell, 1) + offset == coarse
            return jnp.where(inside & match, 0.125, 0.0)

        def restrict(lv, buf, offset):
            nx, ny = halve(lv, buf)
            return nx, ny, dot(ref[None, "half"][pl.ds(0, up8(nx * ny)), :], pair_matrix(lv, offset))

        def spread(nx, ny, value, coarse, buf):
            scratch_ref = ref[None, "half"]
            scratch_ref[pl.ds(0, up8(nx * ny)), :] = value
            for x in range(nx):
                buf[pl.ds(coarse.row(x, 0), ny), :] = scratch_ref[pl.ds(x * ny, ny), :]

        def stretch(cell, offset):
            coarse = iota((LANES, LANES), 0) - offset
            parent = lax.shift_right_arithmetic(cell, 1)
            other = parent + 2 * (cell & 1) - 1
            return jnp.where(coarse == parent, 0.75, 0.0) + jnp.where(coarse == other, 0.25, 0.0)

        def prolong(rows, pitch, origin, weights, value, fine, buf):
            t, te, to = ref[None, "t"], ref[None, "te"], ref[None, "to"]
            t[pl.ds(0, rows), :] = dot(value, weights)
            reach = fine.h // 2
            x0, nx, ny = -reach, fine.nx // 2 + 2 * reach, fine.ny // 2 + 2 * reach
            low = origin + x0 * pitch - reach - 1
            n = (nx - 1) * pitch + ny + 2
            mid = 0.75 * t[pl.ds(low, n), :]
            te[pl.ds(0, n), :] = mid + 0.25 * t[pl.ds(low - pitch, n), :]
            to[pl.ds(0, n), :] = mid + 0.25 * t[pl.ds(low + pitch, n), :]
            for x in range(nx):
                for px, src in ((0, te), (1, to)):
                    at = x * pitch + 1
                    mid = 0.75 * src[pl.ds(at, ny), :]
                    to_row = fine.row(2 * (x + x0) + px, -2 * reach)
                    buf[pl.ds(to_row, ny, stride=2), :] = mid + 0.25 * src[pl.ds(at - 1, ny), :]
                    buf[pl.ds(to_row + 1, ny, stride=2), :] = mid + 0.25 * src[pl.ds(at + 1, ny), :]

        def columns(fine):
            return iota((LANES, LANES), 1) - fine.zo

        def depth_copy(which, k):
            return pltpu.make_async_remote_copy(
                src_ref=ref[None, "zs"].at[which],
                dst_ref=ref[None, "zr"].at[which, gz],
                send_sem=ref[None, "zsend"].at[which, k],
                recv_sem=ref[None, "zrecv"].at[which, k],
                device_id=(gx, gy, depth_peer(k)),
                device_id_type=MESH,
            )

        def depth_arrival(which, k):
            source = lax.rem(gz + gzn - k, gzn)
            return pltpu.make_async_remote_copy(
                src_ref=ref[None, "zs"].at[which],
                dst_ref=ref[None, "zr"].at[which, source],
                send_sem=ref[None, "zsend"].at[which, k],
                recv_sem=ref[None, "zrecv"].at[which, k],
                device_id=(gx, gy, depth_peer(k)),
                device_id_type=MESH,
            )

        def plane_copy(which, i, j):
            px, py = plane_peer(i, j)
            return pltpu.make_async_remote_copy(
                src_ref=ref[None, "ps"].at[which],
                dst_ref=ref[None, "pr"].at[which, gx * gyn + gy],
                send_sem=ref[None, "psend"].at[which, i * gyn + j],
                recv_sem=ref[None, "precv"].at[which, i * gyn + j],
                device_id=(px, py, gz),
                device_id_type=MESH,
            )

        def plane_arrival(which, i, j):
            sx, sy = lax.rem(gx + gxn - i, gxn), lax.rem(gy + gyn - j, gyn)
            px, py = plane_peer(i, j)
            return pltpu.make_async_remote_copy(
                src_ref=ref[None, "ps"].at[which],
                dst_ref=ref[None, "pr"].at[which, sx * gyn + sy],
                send_sem=ref[None, "psend"].at[which, i * gyn + j],
                recv_sem=ref[None, "precv"].at[which, i * gyn + j],
                device_id=(px, py, gz),
                device_id_type=MESH,
            )

        def gather_depth_start(which, block):
            ref[None, "zs"][which] = block[:blk]
            for k in range(1, gzn):
                depth_copy(which, k).start()

        def gather_plane_start(which):
            total = ref[None, "zs"][which]
            for k in range(1, gzn):
                depth_arrival(which, k).wait_recv()
            for k in range(1, gzn):
                total = total + ref[None, "zr"][which, lax.rem(gz + k, gzn)]
            ref[None, "ps"][which] = total
            for i, j in plane_peers:
                plane_copy(which, i, j).start()
            ref[None, "pr"][which, gx * gyn + gy] = total

        def gather_end(which, buf):
            for i, j in plane_peers:
                plane_arrival(which, i, j).wait_recv()
            for i in range(gxn):
                for x in range(cx):
                    for y in range(cy):
                        rows = [ref[None, "pr"][which, i * gyn + j, pl.ds(x * cy + y, 1), :] for j in range(gyn)]
                        at = three.row(i * cx + x, y)
                        buf[pl.ds(at, gyn, stride=cy), :] = jnp.concatenate(rows, axis=0)

        def gather_waits():
            for which in range(2):
                for k in range(1, gzn):
                    depth_copy(which, k).wait_send()
                for i, j in plane_peers:
                    plane_copy(which, i, j).wait_send()

        first, middle, last = local
        for x in range(first.nx):
            ref[0, "v"][pl.ds(first.row(x, 0), first.ny), :] = k_ref[x]
            ref[0, "w"][pl.ds(first.row(x, 0), first.ny), :] = b_ref[x]
        for fine, coarse in ((first, middle), (middle, last)):
            nx, ny, value = restrict(fine, ref[fine.index, "v"], coarse.zo)
            spread(nx, ny, value, coarse, ref[coarse.index, "v"])
        _, _, k_block = restrict(last, ref[2, "v"], gz * cz + three.zo)

        pl.semaphore_wait(barrier, len(plane_peers) + gzn - 1 + len(diagonal))
        slot0 = begin_faces(first, ref[0, "v"])
        gather_depth_start(0, k_block)
        slot1 = begin_deep(middle, ref[1, "v"])
        slot2 = begin_deep(last, ref[2, "v"])
        halo = end_faces(first, ref[0, "v"], slot0)
        prepare(first, ref[0, "v"], halo)

        def load(lv):
            ref[lv.index, "r"][...] = ref[lv.index, "w"][pl.ds(lv.c0, lv.n), :] * ref[lv.index, "iv"][...]

        def residual(lv, name):
            ref[lv.index, name][pl.ds(lv.c0, lv.n), :] = ref[lv.index, "r"][...] * ref[lv.index, "dg"][...]

        load(first)
        sweeps(first, None, STEPS, True)
        residual(first, "w")
        nx, ny, value = restrict(first, ref[0, "w"], middle.zo)
        spread(nx, ny, value, middle, ref[1, "w"])
        slot = begin_deep(middle, ref[1, "w"])
        end_deep(middle, ref[1, "v"], slot1)
        prepare(middle, ref[1, "v"], None)
        gather_plane_start(0)
        end_deep(middle, ref[1, "w"], slot)
        load(middle)
        sweeps(middle, None, STEPS, True)
        residual(middle, "w")
        nx, ny, value = restrict(middle, ref[1, "w"], last.zo)
        spread(nx, ny, value, last, ref[2, "w"])
        slot = begin_deep(last, ref[2, "w"])
        ref[1, "v"][pl.ds(middle.c0, middle.n), :] = ref[1, "r"][...]
        slot1 = begin_deep(middle, ref[1, "v"])
        end_deep(last, ref[2, "v"], slot2)
        prepare(last, ref[2, "v"], None)
        end_deep(last, ref[2, "w"], slot)
        load(last)
        sweeps(last, None, STEPS, True)
        residual(last, "w")
        _, _, b_block = restrict(last, ref[2, "w"], gz * cz + three.zo)
        gather_depth_start(1, b_block)
        ref[2, "v"][pl.ds(last.c0, last.n), :] = ref[2, "r"][...]
        slot2 = begin_deep(last, ref[2, "v"])
        gather_end(0, ref[3, "v"])
        prepare(three, ref[3, "v"], None)
        gather_plane_start(1)
        nx, ny, value = restrict(three, ref[3, "v"], four.zo)
        spread(nx, ny, value, four, ref[4, "v"])
        prepare(four, ref[4, "v"], None)
        end_deep(middle, ref[1, "v"], slot1)
        end_deep(last, ref[2, "v"], slot2)
        for lv in (middle, last):
            ref[lv.index, "r"][...] = ref[lv.index, "v"][pl.ds(lv.c0, lv.n), :]
        gather_end(1, ref[3, "w"])

        load(three)
        sweeps(three, None, STEPS, True)
        residual(three, "w")
        nx, ny, value = restrict(three, ref[3, "w"], four.zo)
        spread(nx, ny, value, four, ref[4, "w"])
        load(four)
        sweeps(four, None, COARSE_STEPS, False)

        def lift(lv):
            span = pl.ds(lv.c0, lv.n)
            ref[lv.index, "v"][span, :] = jnp.where(ref[lv.index, "iv"][...] > 0.0, ref[lv.index, "v"][span, :], 0.0)
            sweeps(lv, ref[lv.index, "v"], STEPS, lv.index == 0)

        def solved(lv):
            ref[lv.index, "w"][pl.ds(lv.c0, lv.n), :] = ref[lv.index, "u"][...]
            return ref[lv.index, "w"]

        field = solved(four)
        prolong(four.rows, four.pitch, four.row(0, 0), stretch(columns(three), four.zo), field[...], three, ref[3, "v"])
        lift(three)
        field = solved(three)

        reach = HALO // 2 + 1
        pitch = cy + 2 * reach
        picked = up8((cx + 2 * reach) * pitch)
        row, source = iota((picked, three.rows), 0), iota((picked, three.rows), 1)
        plane = row // pitch
        cell_x, cell_y = gx * cx - reach + plane, gy * cy - reach + (row - plane * pitch)
        inside = (cell_x >= 0) & (cell_x < three.nx) & (cell_y >= 0) & (cell_y < three.ny)
        wanted = three.row(0, 0) + cell_x * three.pitch + cell_y
        window = dot(jnp.where(inside & (source == wanted), 1.0, 0.0), field[...])
        weights = stretch(columns(last) + gz * last.nz, three.zo)
        prolong(picked, pitch, reach * pitch + reach, weights, window, last, ref[2, "v"])
        lift(last)
        field = solved(last)
        end_deep(last, field, begin_deep(last, field))
        weights = stretch(columns(middle), last.zo)
        prolong(last.rows, last.pitch, last.row(0, 0), weights, field[...], middle, ref[1, "v"])
        lift(middle)
        field = solved(middle)
        end_deep(middle, field, begin_deep(middle, field))
        weights = stretch(columns(first), middle.zo)
        prolong(middle.rows, middle.pitch, middle.row(0, 0), weights, field[...], first, ref[0, "v"])
        sweeps(first, ref[0, "v"], STEPS, True)

        for x in range(first.nx):
            span = pl.ds(first.row(x, 0) - first.c0, first.ny)
            u_ref[x] = ref[0, "u"][span, :]
            res_ref[x] = ref[0, "r"][span, :] * ref[0, "dg"][span, :]

        for slot in range(counters[0]):
            for way in range(6):

                @pl.when(has[way])
                def _():
                    link(first, slot, way).wait_send()

        for lv in (middle, last):
            for slot in range(counters[lv.index]):
                for offset in OFFSETS:

                    @pl.when(exists[offset])
                    def _():
                        deep_link(lv, slot, offset, False).wait_send()

        gather_waits()

    def on_device(right_side, conductivity):
        out = jax.ShapeDtypeStruct(box, jnp.float32)
        return pl.pallas_call(
            kernel,
            out_shape=(out, out),
            in_specs=[pl.BlockSpec(memory_space=pltpu.VMEM)] * 2,
            out_specs=[pl.BlockSpec(memory_space=pltpu.VMEM)] * 2,
            scratch_shapes=shapes,
            compiler_params=pltpu.CompilerParams(
                collective_id=0, has_side_effects=True, vmem_limit_bytes=48 * 1024 * 1024
            ),
        )(right_side, conductivity)

    return on_device


def solution(mesh):
    sizes = tuple(mesh.shape[axis] for axis in ("gx", "gy", "gz"))
    spec = P("gx", "gy", "gz")
    return jax.shard_map(
        build(sizes, (32, 16, 128)), mesh=mesh, in_specs=(spec, spec), out_specs=(spec, spec), check_vma=False
    )
```

time: 116 us -> 80.3 us (0.69)
  Pallas kernels: 112 us -> 76.2 us
    pallas_call x1, Pallas kernels: 112 us -> 76.2 us  [on_device(): pl.pallas_call(kernel, out_shape=(out, out), in_specs=[pl.BlockSpec(memor...]
where the time goes in v1:
time: 80.3 us; the launch traced here: 80.2 us
  Pallas kernels  76.2 us (95%)
  local copies, waits for them, and re-layouts  3.3 us (4%)
    pallas_call x1, Pallas kernels, on_device(): pl.pallas_call(kernel, out_shape=(out, out), in_specs=[pl.BlockSpec(memor...  76.2 us
    unnamed x6, local copies, waits for them, and re-layouts  3.3 us

profile of v1, /device:TPU:1, one launch (start us, length us, event | category | flops | bytes accessed | tf_op | source)
XLA Modules:
  0.0 80.2 jit_solution(6467254931491705583)
XLA Ops:
  0.6 0.0 copy-start
  0.6 0.9 %copy-done = f32[32,16,128]{2,1,0:T(8,128)S(1)} copy-done((f32[32,16,128]{2,1,0:T(8,128)S(1)}, f32[32,16,128]{2,1,0:T(8,128)}, u32[]{:S(2)}) %copy-start) | copy-done | bytes 262168
  1.6 0.0 copy-start.1
  1.6 0.9 %copy-done.1 = f32[32,16,128]{2,1,0:T(8,128)S(1)} copy-done((f32[32,16,128]{2,1,0:T(8,128)S(1)}, f32[32,16,128]{2,1,0:T(8,128)}, u32[]{:S(2)}) %copy-start.1) | copy-done | bytes 262168
  2.5 76.2 %shard_map.41 = (f32[32,16,128]{2,1,0:T(8,128)S(1)}, f32[32,16,128]{2,1,0:T(8,128)S(1)}) custom-call(f32[32,16,128]{2,1,0:T(8,128)S(1)} %copy-done, f32[32,16,128]{2,1,0:T(8,128)S(1)} %copy-done.1), custom_call_target="tpu_custom_call" | custom-call | tf_op jit(solution)/shard_map/pallas_call | solution.py:747
  78.8 0.7 copy.6
  79.5 0.7 copy.7
Async XLA Ops:
  0.6 1.0 %copy-start = (f32[32,16,128]{2,1,0:T(8,128)S(1)}, f32[32,16,128]{2,1,0:T(8,128)}, u32[]{:S(2)}) copy-start(f32[32,16,128]{2,1,0:T(8,128)} %b_ref.1) | copy-start | bytes 786436
  1.6 0.9 %copy-start.1 = (f32[32,16,128]{2,1,0:T(8,128)S(1)}, f32[32,16,128]{2,1,0:T(8,128)}, u32[]{:S(2)}) copy-start(f32[32,16,128]{2,1,0:T(8,128)} %k_ref.1) | copy-start | bytes 786436

commit v2 on v1

--- a/solution.py
+++ b/solution.py
@@ -11,7 +11,6 @@
 UPPER_EDGE = 2.0
 MESH = pl.DeviceIdType.MESH
 LANES = 128
-EXCHANGES = 8
 DEEP = 4
 HALO = 4
 OFFSETS = [(i, j, k) for i in (-1, 0, 1) for j in (-1, 0, 1) for k in (-1, 0, 1) if i or j or k]
@@ -45,9 +44,9 @@
         self.zo = 0 if nz == LANES else h
         self.factor = 0.25**index
         self.wide = nz == LANES and not shared
-        self.deep = h > 1
-        self.chunks = self.n // 8
-        self.half = -(-self.chunks // 2)
+        self.per = LANES // (2 * h)
+        self.halves, self.parts = up8(ny) // 8, -(-nx // self.per)
+        self.sends = not shared
 
     def row(self, x, y):
         return self.c0 + (x + self.h - 1) * self.pitch + y + self.h
@@ -57,31 +56,24 @@
         padded = pltpu.VMEM((self.rows, LANES), jnp.float32)
         shapes = {name: field for name in ("xm", "xp", "ym", "yp", "zm", "zp", "dg", "iv", "r", "u")}
         shapes.update({name: padded for name in ("d0", "d1", "v", "w")})
-        count = EXCHANGES
-        if self.deep:
+        if self.sends:
             for name in ("s", "q"):
                 shapes[name + "x"] = pltpu.VMEM((DEEP, 2, self.h * self.ny, LANES), jnp.float32)
                 shapes[name + "y"] = pltpu.VMEM((DEEP, 2, self.h * self.nx, LANES), jnp.float32)
                 shapes[name + "c"] = pltpu.VMEM((DEEP, 4, self.h * self.h, LANES), jnp.float32)
-            shapes["sz"] = pltpu.VMEM((DEEP, 8, LANES), jnp.float32)
-            shapes["qz"] = pltpu.VMEM((DEEP, 18, 8, LANES), jnp.float32)
-            shapes["zone"] = pltpu.VMEM((6, up8(self.pitch), LANES), jnp.float32)
+            shapes["sz"] = pltpu.VMEM((DEEP, self.halves, self.parts, 8, LANES), jnp.float32)
+            shapes["qz"] = pltpu.VMEM((DEEP, 18, self.halves, self.parts, 8, LANES), jnp.float32)
+            shapes["zone"] = pltpu.VMEM((2 * (2 + self.parts), up8(self.pitch), LANES), jnp.float32)
             shapes["send"] = pltpu.SemaphoreType.DMA((DEEP, 26))
             shapes["recv"] = pltpu.SemaphoreType.DMA((DEEP, 26))
-        elif not self.shared:
-            for name in ("s", "q"):
-                shapes[name + "x"] = pltpu.VMEM((count, 2, self.ny, LANES), jnp.float32)
-                shapes[name + "y"] = pltpu.VMEM((count, 2, self.nx, LANES), jnp.float32)
-            shapes["sz"] = pltpu.VMEM((count, 16, LANES), jnp.float32)
-            shapes["qz"] = pltpu.VMEM((count, 2, 16, LANES), jnp.float32)
-            shapes["send"] = pltpu.SemaphoreType.DMA((count, 6))
-            shapes["recv"] = pltpu.SemaphoreType.DMA((count, 6))
         return shapes
 
-    def groups(self):
-        count = -(-self.n // 96)
-        size = up8(-(-self.n // count))
-        return [(lo, min(size, self.n - lo)) for lo in range(0, self.n, size)]
+    def groups(self, skip=0):
+        skip = skip * self.pitch if self.h > 1 else 0
+        first, last = skip, self.n - skip
+        count = -(-(last - first) // 96)
+        size = up8(-(-(last - first) // count))
+        return [(lo, min(size, last - lo)) for lo in range(first, last, size)]
 
 
 def dot(a, b):
@@ -100,11 +92,13 @@
 def build(mesh_shape, box):
     gxn, gyn, gzn = mesh_shape
     bx, by, bz = box
-    local = [Level(i, bx >> i, by >> i, bz >> i, HALO if i else 1, False) for i in range(3)]
+    local = [Level(i, bx >> i, by >> i, bz >> i, HALO, False) for i in range(3)]
+    rim = Level(0, bx, by, 4 * HALO, HALO, False)
+    rim.index, rim.sends = "rim", False
     cx, cy, cz = bx >> 3, by >> 3, bz >> 3
     three = Level(3, gxn * cx, gyn * cy, gzn * cz, 1, True)
     four = Level(4, three.nx // 2, three.ny // 2, three.nz // 2, 1, True)
-    levels = local + [three, four]
+    levels = local + [rim, three, four]
     blk = cx * cy
     names = [(lv.index, name) for lv in levels for name in lv.scratch()]
     shapes = [shape for lv in levels for shape in lv.scratch().values()]
@@ -128,16 +122,6 @@
     def kernel(b_ref, k_ref, u_ref, res_ref, *scratch):
         ref = {key: value for key, value in zip(names, scratch)}
         gx, gy, gz = lax.axis_index("gx"), lax.axis_index("gy"), lax.axis_index("gz")
-        has = (gx > 0, gx < gxn - 1, gy > 0, gy < gyn - 1, gz > 0, gz < gzn - 1)
-        peer = (
-            (gx - 1, gy, gz),
-            (gx + 1, gy, gz),
-            (gx, gy - 1, gz),
-            (gx, gy + 1, gz),
-            (gx, gy, gz - 1),
-            (gx, gy, gz + 1),
-        )
-        lane = iota((8, LANES), 1)
         plane_peers = [(i, j) for i in range(gxn) for j in range(gyn) if i or j]
 
         def plane_peer(i, j):
@@ -149,8 +133,8 @@
         for lv in levels:
             for name in ("d0", "d1", "v", "w"):
                 ref[lv.index, name][...] = jnp.zeros((lv.rows, LANES), jnp.float32)
-            if not lv.shared:
-                for name in ("qx", "qy", "qz") + (("qc",) if lv.deep else ()):
+            if lv.sends:
+                for name in ("qx", "qy", "qz", "qc"):
                     target = ref[lv.index, name]
                     target[...] = jnp.zeros(target.shape, jnp.float32)
 
@@ -184,88 +168,6 @@
             around_edge = tuple(lax.rem(at[a] + offset[a] + sizes[a], sizes[a]) for a in range(3))
             pl.semaphore_signal(barrier, inc=1, device_id=around_edge, device_id_type=MESH)
 
-        def link(lv, slot, way):
-            axis, side = "xyz"[way // 2], way % 2
-            source = ref[lv.index, "s" + axis].at[slot]
-            if axis != "z":
-                source = source.at[side]
-            return pltpu.make_async_remote_copy(
-                src_ref=source,
-                dst_ref=ref[lv.index, "q" + axis].at[slot, 1 - side],
-                send_sem=ref[lv.index, "send"].at[slot, way],
-                recv_sem=ref[lv.index, "recv"].at[slot, way ^ 1],
-                device_id=peer[way],
-                device_id_type=MESH,
-            )
-
-        def incoming(lv, slot, way):
-            axis, side = "xyz"[way // 2], way % 2
-            source = ref[lv.index, "s" + axis].at[slot]
-            if axis != "z":
-                source = source.at[side]
-            return pltpu.make_async_remote_copy(
-                src_ref=source,
-                dst_ref=ref[lv.index, "q" + axis].at[slot, side],
-                send_sem=ref[lv.index, "send"].at[slot, way],
-                recv_sem=ref[lv.index, "recv"].at[slot, way],
-                device_id=peer[way],
-                device_id_type=MESH,
-            )
-
-        def start(lv, slot, ways):
-            for way in ways:
-
-                @pl.when(has[way])
-                def _():
-                    link(lv, slot, way).start()
-
-        def finish(lv, slot, ways):
-            for way in ways:
-
-                @pl.when(has[way])
-                def _():
-                    incoming(lv, slot, way).wait_recv()
-
-        def begin_faces(lv, buf):
-            slot = counters[lv.index]
-            counters[lv.index] += 1
-            out = ref[lv.index, "sx"]
-            out[slot, 0] = buf[pl.ds(lv.row(0, 0), lv.ny), :]
-            out[slot, 1] = buf[pl.ds(lv.row(lv.nx - 1, 0), lv.ny), :]
-            start(lv, slot, (0, 1))
-            out = ref[lv.index, "sy"]
-            out[slot, 0] = buf[pl.ds(lv.row(0, 0), lv.nx, stride=lv.pitch), :]
-            out[slot, 1] = buf[pl.ds(lv.row(0, lv.ny - 1), lv.nx, stride=lv.pitch), :]
-            start(lv, slot, (2, 3))
-            out = ref[lv.index, "sz"]
-            packed = jnp.zeros((8, LANES), jnp.float32)
-            for c in range(lv.chunks):
-                cc = c % lv.half
-                value = buf[pl.ds(lv.c0 + 8 * c, 8), :]
-                packed = jnp.where(lane >= 2 * cc, roll(value, 2 * cc + 1), packed)
-                if cc == lv.half - 1 or c == lv.chunks - 1:
-                    out[slot, pl.ds(8 * (c // lv.half), 8), :] = packed
-            start(lv, slot, (4, 5))
-            return slot
-
-        def end_faces(lv, buf, slot):
-            finish(lv, slot, range(6))
-            got = ref[lv.index, "qx"]
-            buf[pl.ds(lv.row(-1, 0), lv.ny), :] = got[slot, 0]
-            buf[pl.ds(lv.row(lv.nx, 0), lv.ny), :] = got[slot, 1]
-            got = ref[lv.index, "qy"]
-            buf[pl.ds(lv.row(0, -1), lv.nx, stride=lv.pitch), :] = got[slot, 0]
-            buf[pl.ds(lv.row(0, lv.ny), lv.nx, stride=lv.pitch), :] = got[slot, 1]
-            got = ref[lv.index, "qz"]
-            even = lane % 2 == 0
-            return [
-                jnp.where(even, got[slot, 0, pl.ds(8 * h, 8), :], roll(got[slot, 1, pl.ds(8 * h, 8), :], -2))
-                for h in range(2)
-            ]
-
-        def faces(lv, buf):
-            return end_faces(lv, buf, begin_faces(lv, buf)) if lv.wide else None
-
         def deep_link(lv, slot, offset, arriving):
             i, j, k = offset
             sent = OFFSETS.index(offset)
@@ -273,7 +175,11 @@
 
             def part(kind, which):
                 if k:
-                    return ref[lv.index, kind + "z"].at[(slot,) if which is None else (slot, which)]
+                    way_x, way_y = (-i, -j) if arriving else (i, j)
+                    rows = pl.ds(0, lv.halves) if not way_y else pl.ds(0 if way_y < 0 else lv.halves - 1, 1)
+                    planes = pl.ds(0, lv.parts) if not way_x else pl.ds(0 if way_x < 0 else lv.parts - 1, 1)
+                    index = (slot,) if which is None else (slot, which)
+                    return ref[lv.index, kind + "z"].at[index + (rows, planes)]
                 name = "c" if i and j else "x" if i else "y"
                 return ref[lv.index, kind + name].at[slot, which]
 
@@ -317,16 +223,19 @@
             counters[lv.index] += 1
             h, nx, ny, nz = lv.h, lv.nx, lv.ny, lv.nz
             out = ref[lv.index, "sz"]
-            packed = jnp.zeros((ny, LANES), jnp.float32)
-            where = iota((ny, LANES), 1)
-            for x in range(nx):
-                value = buf[pl.ds(lv.row(x, 0), ny), :]
-                low = 2 * h * x
-                packed = jnp.where(where >= low, roll(value, low - h), packed)
-                packed = jnp.where(where >= low + h, roll(value, low + h - nz), packed)
-            out[slot, pl.ds(0, ny), :] = packed
-            if ny < 8:
-                out[slot, pl.ds(ny, 8 - ny), :] = packed[: 8 - ny]
+            size = min(ny, 8)
+            where = iota((size, LANES), 1)
+            for part in range(lv.parts):
+                for half in range(lv.halves):
+                    packed = jnp.zeros((size, LANES), jnp.float32)
+                    for x in range(part * lv.per, min(nx, (part + 1) * lv.per)):
+                        value = buf[pl.ds(lv.row(x, 8 * half), size), :]
+                        low = 2 * h * (x % lv.per)
+                        packed = jnp.where(where >= low, roll(value, low - lv.zo), packed)
+                        packed = jnp.where(where >= low + h, roll(value, low + 2 * h - nz - lv.zo), packed)
+                    out[slot, half, part, pl.ds(0, size), :] = packed
+                    if size < 8:
+                        out[slot, half, part, pl.ds(size, 8 - size), :] = packed[: 8 - size]
             deep_start(lv, slot, EDGES)
             for side in (-1, 1):
                 x0, y0 = near_side(nx, side, h), near_side(ny, side, h)
@@ -345,8 +254,8 @@
             deep_start(lv, slot, [offset for offset in OFFSETS if not offset[2]])
             return slot
 
-        def end_deep(lv, buf, slot):
-            h, nx, ny, nz = lv.h, lv.nx, lv.ny, lv.nz
+        def end_deep(lv, buf, slot, target=None):
+            h, nx, ny, nz = lv.h, lv.nx, lv.ny, lv.nz if target is None else rim.nz
             deep_finish(lv, slot, [offset for offset in OFFSETS if not offset[2]])
             for side in (-1, 1):
                 x0, y0 = far_side(nx, side, h), far_side(ny, side, h)
@@ -364,66 +273,72 @@
                         ]
             deep_finish(lv, slot, EDGES)
             got, zone = ref[lv.index, "qz"], ref[lv.index, "zone"]
-            for i in (-1, 0, 1):
-                for k in (-1, 1):
-                    place = 2 * (i + 1) + (k > 0)
-                    zone[place, pl.ds(0, h), :] = got[slot, EDGES.index((i, -1, k)), pl.ds(ny - h, h), :]
-                    middle = (i, 0, k)
-                    zone[place, pl.ds(h, ny), :] = got[slot, EDGES.index(middle), pl.ds(0, ny), :]
-                    zone[place, pl.ds(h + ny, h), :] = got[slot, EDGES.index((i, 1, k)), pl.ds(0, h), :]
+            sources = [(-1, lv.parts - 1)] + [(0, part) for part in range(lv.parts)] + [(1, 0)]
+            size = min(ny, 8)
+            for place, (i, part) in enumerate(sources):
+                for k in (0, 1):
+                    side = 2 * k - 1
+                    into = zone.at[2 * place + k]
+                    into[pl.ds(0, h), :] = got[
+                        slot, EDGES.index((i, -1, side)), lv.halves - 1, part, pl.ds(size - h, h), :
+                    ]
+                    for half in range(lv.halves):
+                        into[pl.ds(h + 8 * half, size), :] = got[
+                            slot, EDGES.index((i, 0, side)), half, part, pl.ds(0, size), :
+                        ]
+                    into[pl.ds(h + ny, h), :] = got[slot, EDGES.index((i, 1, side)), 0, part, pl.ds(0, h), :]
             where = iota((lv.pitch, LANES), 1)
             edge = (where < h) | ((where >= nz + h) & (where < nz + 2 * h))
             high = (where & (2 * h - 1)) >= h
-            for i in (-1, 0, 1):
-                low, up = (zone[2 * (i + 1) + k, pl.ds(0, lv.pitch), :] for k in (0, 1))
+            for place, (i, part) in enumerate(sources):
+                low, up = (zone[2 * place + k, pl.ds(0, lv.pitch), :] for k in (0, 1))
                 merged = jnp.where(high, low, roll(up, nz + 2 * h))
-                planes = range(nx) if i == 0 else range(-h, 0) if i < 0 else range(nx, nx + h)
+                if i:
+                    planes = range(-h, 0) if i < 0 else range(nx, nx + h)
+                else:
+                    planes = range(part * lv.per, min(nx, (part + 1) * lv.per))
                 for x in planes:
                     span = pl.ds(lv.row(x, -h), lv.pitch)
-                    buf[span, :] = jnp.where(edge, roll(merged, -(2 * h * (x - i * nx) + h)), buf[span, :])
-
-        def sides(lv, mid, lo, rows, halo):
-            below, above = roll(mid, 1), roll(mid, -1)
-            if lv.wide:
-                edge = jnp.concatenate(
-                    [
-                        roll(halo[c // lv.half], -2 * (c % lv.half))
-                        for c in range(lo // 8, (lo + rows) // 8)
-                    ],
-                    axis=0,
-                )
-                where = iota((rows, LANES), 1)
-                below = jnp.where(where == 0, edge, below)
-                above = jnp.where(where == LANES - 1, edge, above)
-            return below, above
-
-        def around(lv, buf, lo, rows, halo):
+                    shifted = roll(merged, -(2 * h * ((x - i * nx) % lv.per) + h))
+                    if target is None:
+                        buf[span, :] = jnp.where(edge, shifted, buf[span, :])
+                    else:
+                        inner = buf[span, :]
+                        inner = jnp.where(where < 3 * h, roll(inner, h), roll(inner, 5 * h))
+                        inner = jnp.where(edge, shifted, inner)
+                        target[span, :] = jnp.where(where < nz + 2 * h, inner, 0.0)
+
+        def joined(inner, outer):
+            where = iota(inner.shape, 1)
+            outer = jnp.where(where < LANES // 2, roll(outer, -HALO), roll(outer, LANES - 5 * HALO))
+            return jnp.where((where < HALO) | (where >= LANES - HALO), outer, inner)
+
+        def around(lv, buf, lo, rows):
             base = lv.c0 + lo
             mid = buf[pl.ds(base, rows), :]
-            below, above = sides(lv, mid, lo, rows, halo)
             return mid, (
                 buf[pl.ds(base - lv.pitch, rows), :],
                 buf[pl.ds(base + lv.pitch, rows), :],
                 buf[pl.ds(base - 1, rows), :],
                 buf[pl.ds(base + 1, rows), :],
-                below,
-                above,
+                roll(mid, 1),
+                roll(mid, -1),
             )
 
         coeff_names = ("xm", "xp", "ym", "yp", "zm", "zp")
 
-        def applied(lv, buf, lo, rows, halo):
-            mid, near = around(lv, buf, lo, rows, halo)
+        def applied(lv, buf, lo, rows):
+            mid, near = around(lv, buf, lo, rows)
             span = pl.ds(lo, rows)
             total = mid
             for name, value in zip(coeff_names, near):
                 total = total - ref[lv.index, name][span, :] * value
             return mid, total
 
-        def prepare(lv, buf, halo):
+        def prepare(lv, buf):
             for lo, rows in lv.groups():
                 span = pl.ds(lo, rows)
-                mid, near = around(lv, buf, lo, rows, halo)
+                mid, near = around(lv, buf, lo, rows)
                 where = iota((rows, LANES), 1)
                 near = list(near)
                 if lv.shared and lv.nz == LANES:
@@ -448,15 +363,18 @@
             r, u = ref[lv.index, "r"], ref[lv.index, "u"]
             buffers = [ref[lv.index, "d0"], ref[lv.index, "d1"]]
             held = src
+            applications = count - 1 + (src is not None) + final
+            skip = lv.h - 1 - applications
             for step in range(count):
                 keep, push = factors[step]
                 target = buffers[step % 2]
-                halo = faces(lv, held) if held is not None else None
-                for lo, rows in lv.groups():
+                if held is not None:
+                    skip += 1
+                for lo, rows in lv.groups(max(skip, 0)):
                     span = pl.ds(lo, rows)
                     value = r[span, :]
                     if held is not None:
-                        mid, change = applied(lv, held, lo, rows, halo)
+                        mid, change = applied(lv, held, lo, rows)
                         value = value - change
                         r[span, :] = value
                     direction = push * value
@@ -471,10 +389,9 @@
                         u[span, :] = u[span, :] + direction
                 held = target
             if final:
-                halo = faces(lv, held)
-                for lo, rows in lv.groups():
+                for lo, rows in lv.groups(max(skip + 1, 0)):
                     span = pl.ds(lo, rows)
-                    mid, change = applied(lv, held, lo, rows, halo)
+                    mid, change = applied(lv, held, lo, rows)
                     r[span, :] = r[span, :] - change
             return held
 
@@ -622,12 +539,15 @@
         _, _, k_block = restrict(last, ref[2, "v"], gz * cz + three.zo)
 
         pl.semaphore_wait(barrier, len(plane_peers) + gzn - 1 + len(diagonal))
-        slot0 = begin_faces(first, ref[0, "v"])
+        slot0 = begin_deep(first, ref[0, "v"])
+        slot = begin_deep(first, ref[0, "w"])
         gather_depth_start(0, k_block)
         slot1 = begin_deep(middle, ref[1, "v"])
         slot2 = begin_deep(last, ref[2, "v"])
-        halo = end_faces(first, ref[0, "v"], slot0)
-        prepare(first, ref[0, "v"], halo)
+        end_deep(first, ref[0, "v"], slot0, ref["rim", "v"])
+        prepare(first, ref[0, "v"])
+        prepare(rim, ref["rim", "v"])
+        end_deep(first, ref[0, "w"], slot, ref["rim", "w"])
 
         def load(lv):
             ref[lv.index, "r"][...] = ref[lv.index, "w"][pl.ds(lv.c0, lv.n), :] * ref[lv.index, "iv"][...]
@@ -635,14 +555,22 @@
         def residual(lv, name):
             ref[lv.index, name][pl.ds(lv.c0, lv.n), :] = ref[lv.index, "r"][...] * ref[lv.index, "dg"][...]
 
-        load(first)
-        sweeps(first, None, STEPS, True)
-        residual(first, "w")
+        for lv in (first, rim):
+            load(lv)
+            sweeps(lv, None, STEPS, True)
+        r0, edge_r = ref[0, "r"], ref["rim", "r"]
+        for lo, rows in first.groups(first.h - 1):
+            span = pl.ds(lo, rows)
+            value = joined(r0[span, :], edge_r[span, :])
+            ref[0, "v"][pl.ds(first.c0 + lo, rows), :] = value
+            diagonal = joined(ref[0, "dg"][span, :], ref["rim", "dg"][span, :])
+            ref[0, "w"][pl.ds(first.c0 + lo, rows), :] = value * diagonal
         nx, ny, value = restrict(first, ref[0, "w"], middle.zo)
         spread(nx, ny, value, middle, ref[1, "w"])
         slot = begin_deep(middle, ref[1, "w"])
+        slot0 = begin_deep(first, ref[0, "v"])
         end_deep(middle, ref[1, "v"], slot1)
-        prepare(middle, ref[1, "v"], None)
+        prepare(middle, ref[1, "v"])
         gather_plane_start(0)
         end_deep(middle, ref[1, "w"], slot)
         load(middle)
@@ -654,7 +582,7 @@
         ref[1, "v"][pl.ds(middle.c0, middle.n), :] = ref[1, "r"][...]
         slot1 = begin_deep(middle, ref[1, "v"])
         end_deep(last, ref[2, "v"], slot2)
-        prepare(last, ref[2, "v"], None)
+        prepare(last, ref[2, "v"])
         end_deep(last, ref[2, "w"], slot)
         load(last)
         sweeps(last, None, STEPS, True)
@@ -664,14 +592,15 @@
         ref[2, "v"][pl.ds(last.c0, last.n), :] = ref[2, "r"][...]
         slot2 = begin_deep(last, ref[2, "v"])
         gather_end(0, ref[3, "v"])
-        prepare(three, ref[3, "v"], None)
+        prepare(three, ref[3, "v"])
         gather_plane_start(1)
         nx, ny, value = restrict(three, ref[3, "v"], four.zo)
         spread(nx, ny, value, four, ref[4, "v"])
-        prepare(four, ref[4, "v"], None)
+        prepare(four, ref[4, "v"])
         end_deep(middle, ref[1, "v"], slot1)
         end_deep(last, ref[2, "v"], slot2)
-        for lv in (middle, last):
+        end_deep(first, ref[0, "v"], slot0, ref["rim", "v"])
+        for lv in (first, rim, middle, last):
             ref[lv.index, "r"][...] = ref[lv.index, "v"][pl.ds(lv.c0, lv.n), :]
         gather_end(1, ref[3, "w"])
 
@@ -686,7 +615,7 @@
         def lift(lv):
             span = pl.ds(lv.c0, lv.n)
             ref[lv.index, "v"][span, :] = jnp.where(ref[lv.index, "iv"][...] > 0.0, ref[lv.index, "v"][span, :], 0.0)
-            sweeps(lv, ref[lv.index, "v"], STEPS, lv.index == 0)
+            sweeps(lv, ref[lv.index, "v"], STEPS, lv.index in (0, "rim"))
 
         def solved(lv):
             ref[lv.index, "w"][pl.ds(lv.c0, lv.n), :] = ref[lv.index, "u"][...]
@@ -716,23 +645,20 @@
         lift(middle)
         field = solved(middle)
         end_deep(middle, field, begin_deep(middle, field))
-        weights = stretch(columns(first), middle.zo)
-        prolong(middle.rows, middle.pitch, middle.row(0, 0), weights, field[...], first, ref[0, "v"])
-        sweeps(first, ref[0, "v"], STEPS, True)
+        column = iota((LANES, LANES), 1)
+        near_low = jnp.where(column < 3 * HALO, column - HALO, column + (LANES - 5 * HALO))
+        for lv, cells in ((first, column), (rim, near_low)):
+            weights = stretch(cells, middle.zo)
+            prolong(middle.rows, middle.pitch, middle.row(0, 0), weights, field[...], lv, ref[lv.index, "v"])
+            lift(lv)
 
         for x in range(first.nx):
             span = pl.ds(first.row(x, 0) - first.c0, first.ny)
-            u_ref[x] = ref[0, "u"][span, :]
-            res_ref[x] = ref[0, "r"][span, :] * ref[0, "dg"][span, :]
-
-        for slot in range(counters[0]):
-            for way in range(6):
-
-                @pl.when(has[way])
-                def _():
-                    link(first, slot, way).wait_send()
-
-        for lv in (middle, last):
+            u_ref[x] = joined(ref[0, "u"][span, :], ref["rim", "u"][span, :])
+            value = joined(ref[0, "r"][span, :], ref["rim", "r"][span, :])
+            res_ref[x] = value * joined(ref[0, "dg"][span, :], ref["rim", "dg"][span, :])
+
+        for lv in (first, middle, last):
             for slot in range(counters[lv.index]):
                 for offset in OFFSETS:
 

time: 80.3 us -> 67.3 us (0.84)
  Pallas kernels: 76.2 us -> 63.2 us
    pallas_call x1, Pallas kernels: 76.2 us -> 63.2 us  [on_device(): pl.pallas_call(kernel, out_shape=(out, out), in_specs=[pl.BlockSpec(memor...]
where the time goes in v2:
time: 67.3 us; the launch traced here: 67.1 us
  Pallas kernels  63.2 us (94%)
  local copies, waits for them, and re-layouts  3.3 us (5%)
    pallas_call x1, Pallas kernels, on_device(): pl.pallas_call(kernel, out_shape=(out, out), in_specs=[pl.BlockSpec(memor...  63.2 us
    unnamed x6, local copies, waits for them, and re-layouts  3.3 us

profile of v2, /device:TPU:1, one launch (start us, length us, event | category | flops | bytes accessed | tf_op | source)
XLA Modules:
  0.0 67.1 jit_solution(8625428797609562199)
XLA Ops:
  0.6 0.0 copy-start
  0.6 0.9 %copy-done = f32[32,16,128]{2,1,0:T(8,128)S(1)} copy-done((f32[32,16,128]{2,1,0:T(8,128)S(1)}, f32[32,16,128]{2,1,0:T(8,128)}, u32[]{:S(2)}) %copy-start) | copy-done | bytes 262168
  1.6 0.0 copy-start.1
  1.6 0.9 %copy-done.1 = f32[32,16,128]{2,1,0:T(8,128)S(1)} copy-done((f32[32,16,128]{2,1,0:T(8,128)S(1)}, f32[32,16,128]{2,1,0:T(8,128)}, u32[]{:S(2)}) %copy-start.1) | copy-done | bytes 262168
  2.5 63.2 %shard_map.41 = (f32[32,16,128]{2,1,0:T(8,128)S(1)}, f32[32,16,128]{2,1,0:T(8,128)S(1)}) custom-call(f32[32,16,128]{2,1,0:T(8,128)S(1)} %copy-done, f32[32,16,128]{2,1,0:T(8,128)S(1)} %copy-done.1), custom_call_target="tpu_custom_call" | custom-call | tf_op jit(solution)/shard_map/pallas_call | solution.py:673
  65.7 0.7 %copy.6 = f32[32,16,128]{2,1,0:T(8,128)} copy(f32[32,16,128]{2,1,0:T(8,128)S(1)} %get-tuple-element.4) | data formatting | bytes 524288
  66.4 0.7 %copy.7 = f32[32,16,128]{2,1,0:T(8,128)} copy(f32[32,16,128]{2,1,0:T(8,128)S(1)} %get-tuple-element.5) | data formatting | bytes 524288
Async XLA Ops:
  0.6 1.0 %copy-start = (f32[32,16,128]{2,1,0:T(8,128)S(1)}, f32[32,16,128]{2,1,0:T(8,128)}, u32[]{:S(2)}) copy-start(f32[32,16,128]{2,1,0:T(8,128)} %b_ref.1) | copy-start | bytes 786436
  1.6 0.9 %copy-start.1 = (f32[32,16,128]{2,1,0:T(8,128)S(1)}, f32[32,16,128]{2,1,0:T(8,128)}, u32[]{:S(2)}) copy-start(f32[32,16,128]{2,1,0:T(8,128)} %k_ref.1) | copy-start | bytes 786436

commit v3 on v2

--- a/solution.py
+++ b/solution.py
@@ -93,7 +93,8 @@
     gxn, gyn, gzn = mesh_shape
     bx, by, bz = box
     local = [Level(i, bx >> i, by >> i, bz >> i, HALO, False) for i in range(3)]
-    rim = Level(0, bx, by, 4 * HALO, HALO, False)
+    slab = bx // 4
+    rim = Level(0, slab, by, 4 * HALO, HALO, False)
     rim.index, rim.sends = "rim", False
     cx, cy, cz = bx >> 3, by >> 3, bz >> 3
     three = Level(3, gxn * cx, gyn * cy, gzn * cz, 1, True)
@@ -107,6 +108,9 @@
         "te": pltpu.VMEM((max(lv.n for lv in levels) + 16, LANES), jnp.float32),
         "to": pltpu.VMEM((max(lv.n for lv in levels) + 16, LANES), jnp.float32),
         "half": pltpu.VMEM((128, LANES), jnp.float32),
+        "kin": pltpu.VMEM(box, jnp.float32),
+        "bin": pltpu.VMEM(box, jnp.float32),
+        "insem": pltpu.SemaphoreType.DMA((2,)),
         "zs": pltpu.VMEM((2, blk, LANES), jnp.float32),
         "zr": pltpu.VMEM((2, gzn, blk, LANES), jnp.float32),
         "ps": pltpu.VMEM((2, blk, LANES), jnp.float32),
@@ -130,13 +134,12 @@
         def depth_peer(k):
             return lax.rem(gz + k, gzn)
 
-        for lv in levels:
-            for name in ("d0", "d1", "v", "w"):
-                ref[lv.index, name][...] = jnp.zeros((lv.rows, LANES), jnp.float32)
-            if lv.sends:
-                for name in ("qx", "qy", "qz", "qc"):
-                    target = ref[lv.index, name]
-                    target[...] = jnp.zeros(target.shape, jnp.float32)
+        fetches = [
+            pltpu.make_async_copy(source, ref[None, name], ref[None, "insem"].at[i])
+            for i, (source, name) in enumerate(((k_ref, "kin"), (b_ref, "bin")))
+        ]
+        for fetch in fetches:
+            fetch.start()
 
         barrier = pltpu.get_barrier_semaphore()
         for i, j in plane_peers:
@@ -146,6 +149,7 @@
             pl.semaphore_signal(barrier, inc=1, device_id=(gx, gy, depth_peer(k)), device_id_type=MESH)
 
         counters = [0, 0, 0]
+        first, middle, last = local
         at = (gx, gy, gz)
         sizes = (gxn, gyn, gzn)
 
@@ -167,6 +171,39 @@
         for offset in diagonal:
             around_edge = tuple(lax.rem(at[a] + offset[a] + sizes[a], sizes[a]) for a in range(3))
             pl.semaphore_signal(barrier, inc=1, device_id=around_edge, device_id_type=MESH)
+
+        for lv in (three, four):
+            for name in ("d0", "d1", "v", "w"):
+                ref[lv.index, name][...] = jnp.zeros((lv.rows, LANES), jnp.float32)
+
+        def clear(lv):
+            for offset in OFFSETS:
+
+                @pl.when(jnp.logical_not(exists[offset]))
+                def _():
+                    name, place = landing(offset)
+                    piece = ref[lv.index, "q" + name].at[:, place]
+                    piece[...] = jnp.zeros(piece.shape, jnp.float32)
+
+        def landing(offset):
+            i, j, k = offset
+            if k:
+                return "z", EDGES.index(offset)
+            if i and j:
+                return "c", 2 * (i > 0) + (j > 0)
+            return ("x", int(i > 0)) if i else ("y", int(j > 0))
+
+        pending = []
+
+        def drain(keep=()):
+            for entry in [entry for entry in pending if entry not in keep]:
+                pending.remove(entry)
+                lv, slot = entry
+                for offset in OFFSETS:
+
+                    @pl.when(exists[offset])
+                    def _():
+                        deep_link(lv, slot, offset, False).wait_send()
 
         def deep_link(lv, slot, offset, arriving):
             i, j, k = offset
@@ -221,6 +258,7 @@
         def begin_deep(lv, buf):
             slot = counters[lv.index]
             counters[lv.index] += 1
+            pending.append((lv, slot))
             h, nx, ny, nz = lv.h, lv.nx, lv.ny, lv.nz
             out = ref[lv.index, "sz"]
             size = min(ny, 8)
@@ -288,37 +326,56 @@
                         ]
                     into[pl.ds(h + ny, h), :] = got[slot, EDGES.index((i, 1, side)), 0, part, pl.ds(0, h), :]
             where = iota((lv.pitch, LANES), 1)
-            edge = (where < h) | ((where >= nz + h) & (where < nz + 2 * h))
             high = (where & (2 * h - 1)) >= h
-            for place, (i, part) in enumerate(sources):
+            merged = []
+            for place in range(len(sources)):
                 low, up = (zone[2 * place + k, pl.ds(0, lv.pitch), :] for k in (0, 1))
-                merged = jnp.where(high, low, roll(up, nz + 2 * h))
-                if i:
-                    planes = range(-h, 0) if i < 0 else range(nx, nx + h)
-                else:
-                    planes = range(part * lv.per, min(nx, (part + 1) * lv.per))
-                for x in planes:
+                merged.append(jnp.where(high, low, roll(up, nz + 2 * h)))
+
+            def shifted(x, more):
+                i = -1 if x < 0 else 1 if x >= nx else 0
+                source = (x - i * nx) % lv.per
+                chosen = merged[0 if i < 0 else len(sources) - 1 if i > 0 else 1 + x // lv.per]
+                return roll(chosen, more - (2 * h * source + h))
+
+            if target is None:
+                edge = (where < h) | ((where >= nz + h) & (where < nz + 2 * h))
+                for x in range(-h, nx + h):
                     span = pl.ds(lv.row(x, -h), lv.pitch)
-                    shifted = roll(merged, -(2 * h * ((x - i * nx) % lv.per) + h))
-                    if target is None:
-                        buf[span, :] = jnp.where(edge, shifted, buf[span, :])
-                    else:
-                        inner = buf[span, :]
-                        inner = jnp.where(where < 3 * h, roll(inner, h), roll(inner, 5 * h))
-                        inner = jnp.where(edge, shifted, inner)
-                        target[span, :] = jnp.where(where < nz + 2 * h, inner, 0.0)
-
-        def joined(inner, outer):
+                    buf[span, :] = jnp.where(edge, shifted(x, 0), buf[span, :])
+            else:
+                group = where & 31
+                edge = (group < h) | ((group >= nz + h) & (group < nz + 2 * h))
+                for x in range(-h, slab + h):
+                    total = jnp.zeros((lv.pitch, LANES), jnp.float32)
+                    for g in range(4):
+                        inner = buf[pl.ds(lv.row(slab * g + x, -h), lv.pitch), :]
+                        inner = jnp.where(group < 3 * h, roll(inner, h + 32 * g), roll(inner, 5 * h + 32 * g))
+                        inner = jnp.where(edge, shifted(slab * g + x, 32 * g), inner)
+                        total = jnp.where(where >= 32 * g, inner, total)
+                    target[pl.ds(rim.row(x, -h), lv.pitch), :] = jnp.where(group < nz + 2 * h, total, 0.0)
+
+        def joined(name, x, from_y, rows):
+            g = x // slab
+            inner = ref[0, name][pl.ds(first.row(x, from_y) - first.c0, rows), :]
+            outer = ref["rim", name][pl.ds(rim.row(x - g * slab, from_y) - rim.c0, rows), :]
             where = iota(inner.shape, 1)
-            outer = jnp.where(where < LANES // 2, roll(outer, -HALO), roll(outer, LANES - 5 * HALO))
+            outer = jnp.where(
+                where < LANES // 2, roll(outer, -HALO - 32 * g), roll(outer, LANES - 5 * HALO - 32 * g)
+            )
             return jnp.where((where < HALO) | (where >= LANES - HALO), outer, inner)
 
         def around(lv, buf, lo, rows):
-            base = lv.c0 + lo
-            mid = buf[pl.ds(base, rows), :]
+            base, p = lv.c0 + lo, lv.pitch
+            if p % 8 == 0:
+                block = buf[pl.ds(base - p, rows + 2 * p), :]
+                before, mid, after = block[:rows], block[p : p + rows], block[2 * p :]
+            else:
+                mid = buf[pl.ds(base, rows), :]
+                before, after = buf[pl.ds(base - p, rows), :], buf[pl.ds(base + p, rows), :]
             return mid, (
-                buf[pl.ds(base - lv.pitch, rows), :],
-                buf[pl.ds(base + lv.pitch, rows), :],
+                before,
+                after,
                 buf[pl.ds(base - 1, rows), :],
                 buf[pl.ds(base + 1, rows), :],
                 roll(mid, 1),
@@ -362,7 +419,7 @@
             factors = chebyshev_factors(count)
             r, u = ref[lv.index, "r"], ref[lv.index, "u"]
             buffers = [ref[lv.index, "d0"], ref[lv.index, "d1"]]
-            held = src
+            held, late = src, count == 3
             applications = count - 1 + (src is not None) + final
             skip = lv.h - 1 - applications
             for step in range(count):
@@ -380,13 +437,15 @@
                     direction = push * value
                     if step > 0:
                         direction = direction + keep * mid
-                    target[pl.ds(lv.c0 + lo, rows), :] = direction
-                    if step == 0 and src is None:
-                        u[span, :] = direction
-                    elif step == 0:
-                        u[span, :] = u[span, :] + mid + direction
-                    else:
-                        u[span, :] = u[span, :] + direction
+                    padded = pl.ds(lv.c0 + lo, rows)
+                    if late and step == count - 1:
+                        total = direction + mid + target[padded, :]
+                        if src is not None:
+                            total = total + src[padded, :] + u[span, :]
+                        u[span, :] = total
+                    target[padded, :] = direction
+                    if not late:
+                        u[span, :] = direction if step == 0 else u[span, :] + direction
                 held = target
             if final:
                 for lo, rows in lv.groups(max(skip + 1, 0)):
@@ -431,9 +490,9 @@
             other = parent + 2 * (cell & 1) - 1
             return jnp.where(coarse == parent, 0.75, 0.0) + jnp.where(coarse == other, 0.25, 0.0)
 
-        def prolong(rows, pitch, origin, weights, value, fine, buf):
+        def prolong(rows, pitch, origin, value, fine, buf):
             t, te, to = ref[None, "t"], ref[None, "te"], ref[None, "to"]
-            t[pl.ds(0, rows), :] = dot(value, weights)
+            t[pl.ds(0, rows), :] = value
             reach = fine.h // 2
             x0, nx, ny = -reach, fine.nx // 2 + 2 * reach, fine.ny // 2 + 2 * reach
             low = origin + x0 * pitch - reach - 1
@@ -529,10 +588,9 @@
                 for i, j in plane_peers:
                     plane_copy(which, i, j).wait_send()
 
-        first, middle, last = local
+        fetches[0].wait()
         for x in range(first.nx):
-            ref[0, "v"][pl.ds(first.row(x, 0), first.ny), :] = k_ref[x]
-            ref[0, "w"][pl.ds(first.row(x, 0), first.ny), :] = b_ref[x]
+            ref[0, "v"][pl.ds(first.row(x, 0), first.ny), :] = ref[None, "kin"][x]
         for fine, coarse in ((first, middle), (middle, last)):
             nx, ny, value = restrict(fine, ref[fine.index, "v"], coarse.zo)
             spread(nx, ny, value, coarse, ref[coarse.index, "v"])
@@ -540,10 +598,15 @@
 
         pl.semaphore_wait(barrier, len(plane_peers) + gzn - 1 + len(diagonal))
         slot0 = begin_deep(first, ref[0, "v"])
+        fetches[1].wait()
+        for x in range(first.nx):
+            ref[0, "w"][pl.ds(first.row(x, 0), first.ny), :] = ref[None, "bin"][x]
         slot = begin_deep(first, ref[0, "w"])
         gather_depth_start(0, k_block)
         slot1 = begin_deep(middle, ref[1, "v"])
         slot2 = begin_deep(last, ref[2, "v"])
+        for lv in local:
+            clear(lv)
         end_deep(first, ref[0, "v"], slot0, ref["rim", "v"])
         prepare(first, ref[0, "v"])
         prepare(rim, ref["rim", "v"])
@@ -558,17 +621,16 @@
         for lv in (first, rim):
             load(lv)
             sweeps(lv, None, STEPS, True)
-        r0, edge_r = ref[0, "r"], ref["rim", "r"]
-        for lo, rows in first.groups(first.h - 1):
-            span = pl.ds(lo, rows)
-            value = joined(r0[span, :], edge_r[span, :])
-            ref[0, "v"][pl.ds(first.c0 + lo, rows), :] = value
-            diagonal = joined(ref[0, "dg"][span, :], ref["rim", "dg"][span, :])
-            ref[0, "w"][pl.ds(first.c0 + lo, rows), :] = value * diagonal
+        for x in range(0, first.nx, 4):
+            rows = 4 * first.pitch
+            value = joined("r", x, -HALO, rows)
+            ref[0, "v"][pl.ds(first.row(x, -HALO), rows), :] = value
+            ref[0, "w"][pl.ds(first.row(x, -HALO), rows), :] = value * joined("dg", x, -HALO, rows)
         nx, ny, value = restrict(first, ref[0, "w"], middle.zo)
         spread(nx, ny, value, middle, ref[1, "w"])
         slot = begin_deep(middle, ref[1, "w"])
         slot0 = begin_deep(first, ref[0, "v"])
+        drain(pending[-2:])
         end_deep(middle, ref[1, "v"], slot1)
         prepare(middle, ref[1, "v"])
         gather_plane_start(0)
@@ -581,6 +643,7 @@
         slot = begin_deep(last, ref[2, "w"])
         ref[1, "v"][pl.ds(middle.c0, middle.n), :] = ref[1, "r"][...]
         slot1 = begin_deep(middle, ref[1, "v"])
+        drain(pending[-2:])
         end_deep(last, ref[2, "v"], slot2)
         prepare(last, ref[2, "v"])
         end_deep(last, ref[2, "w"], slot)
@@ -622,7 +685,9 @@
             return ref[lv.index, "w"]
 
         field = solved(four)
-        prolong(four.rows, four.pitch, four.row(0, 0), stretch(columns(three), four.zo), field[...], three, ref[3, "v"])
+        prolong(
+            four.rows, four.pitch, four.row(0, 0), dot(field[...], stretch(columns(three), four.zo)), three, ref[3, "v"]
+        )
         lift(three)
         field = solved(three)
 
@@ -636,44 +701,48 @@
         wanted = three.row(0, 0) + cell_x * three.pitch + cell_y
         window = dot(jnp.where(inside & (source == wanted), 1.0, 0.0), field[...])
         weights = stretch(columns(last) + gz * last.nz, three.zo)
-        prolong(picked, pitch, reach * pitch + reach, weights, window, last, ref[2, "v"])
+        prolong(picked, pitch, reach * pitch + reach, dot(window, weights), last, ref[2, "v"])
         lift(last)
         field = solved(last)
-        end_deep(last, field, begin_deep(last, field))
+        slot = begin_deep(last, field)
+        drain(pending[-1:])
+        gather_waits()
+        end_deep(last, field, slot)
         weights = stretch(columns(middle), last.zo)
-        prolong(last.rows, last.pitch, last.row(0, 0), weights, field[...], middle, ref[1, "v"])
+        prolong(last.rows, last.pitch, last.row(0, 0), dot(field[...], weights), middle, ref[1, "v"])
         lift(middle)
         field = solved(middle)
         end_deep(middle, field, begin_deep(middle, field))
+        drain([pending[-1]])
         column = iota((LANES, LANES), 1)
-        near_low = jnp.where(column < 3 * HALO, column - HALO, column + (LANES - 5 * HALO))
-        for lv, cells in ((first, column), (rim, near_low)):
-            weights = stretch(cells, middle.zo)
-            prolong(middle.rows, middle.pitch, middle.row(0, 0), weights, field[...], lv, ref[lv.index, "v"])
-            lift(lv)
+        prolong(
+            middle.rows, middle.pitch, middle.row(0, 0), dot(field[...], stretch(column, middle.zo)), first, ref[0, "v"]
+        )
+        lift(first)
+        group = column & 31
+        cells = jnp.where(group < 3 * HALO, group - HALO, group + (LANES - 5 * HALO))
+        weights = jnp.where(group < 6 * HALO, stretch(cells, middle.zo), 0.0)
+        total, planes = None, slab // 2 + 2 * (HALO // 2 + 1)
+        for g in range(4):
+            part = field[pl.ds(middle.row(slab // 2 * g - HALO // 2 - 1, -HALO), planes * middle.pitch), :]
+            part = dot(part, jnp.where(lax.shift_right_arithmetic(column, 5) == g, weights, 0.0))
+            total = part if total is None else total + part
+        rows = planes * middle.pitch
+        prolong(rows, middle.pitch, (HALO // 2 + 1) * middle.pitch + HALO, total, rim, ref["rim", "v"])
+        lift(rim)
 
         for x in range(first.nx):
-            span = pl.ds(first.row(x, 0) - first.c0, first.ny)
-            u_ref[x] = joined(ref[0, "u"][span, :], ref["rim", "u"][span, :])
-            value = joined(ref[0, "r"][span, :], ref["rim", "r"][span, :])
-            res_ref[x] = value * joined(ref[0, "dg"][span, :], ref["rim", "dg"][span, :])
-
-        for lv in (first, middle, last):
-            for slot in range(counters[lv.index]):
-                for offset in OFFSETS:
-
-                    @pl.when(exists[offset])
-                    def _():
-                        deep_link(lv, slot, offset, False).wait_send()
-
-        gather_waits()
+            u_ref[x] = joined("u", x, 0, first.ny)
+            res_ref[x] = joined("r", x, 0, first.ny) * joined("dg", x, 0, first.ny)
+
+        drain()
 
     def on_device(right_side, conductivity):
         out = jax.ShapeDtypeStruct(box, jnp.float32)
         return pl.pallas_call(
             kernel,
             out_shape=(out, out),
-            in_specs=[pl.BlockSpec(memory_space=pltpu.VMEM)] * 2,
+            in_specs=[pl.BlockSpec(memory_space=pltpu.HBM)] * 2,
             out_specs=[pl.BlockSpec(memory_space=pltpu.VMEM)] * 2,
             scratch_shapes=shapes,
             compiler_params=pltpu.CompilerParams(

time: 67.3 us -> 65.1 us (0.967)
  Pallas kernels: 63.2 us -> 61 us
    pallas_call x1, Pallas kernels: 63.2 us -> 61 us  [on_device(): pl.pallas_call(kernel, out_shape=(out, out), in_specs=[pl.BlockSpec(memor...]
where the time goes in v3:
time: 65.1 us; the launch traced here: 65 us
  Pallas kernels  61 us (94%)
  local copies, waits for them, and re-layouts  3.3 us (5%)
    pallas_call x1, Pallas kernels, on_device(): pl.pallas_call(kernel, out_shape=(out, out), in_specs=[pl.BlockSpec(memor...  61 us
    unnamed x6, local copies, waits for them, and re-layouts  3.3 us

profile of v3, /device:TPU:1, one launch (start us, length us, event | category | flops | bytes accessed | tf_op | source)
XLA Modules:
  0.0 65.0 jit_solution(15587227239631267626)
XLA Ops:
  0.6 0.0 copy-start
  0.6 0.9 %copy-done = f32[32,16,128]{2,1,0:T(8,128)S(1)} copy-done((f32[32,16,128]{2,1,0:T(8,128)S(1)}, f32[32,16,128]{2,1,0:T(8,128)}, u32[]{:S(2)}) %copy-start) | copy-done | bytes 262168
  1.6 0.0 copy-start.1
  1.6 0.9 %copy-done.1 = f32[32,16,128]{2,1,0:T(8,128)S(1)} copy-done((f32[32,16,128]{2,1,0:T(8,128)S(1)}, f32[32,16,128]{2,1,0:T(8,128)}, u32[]{:S(2)}) %copy-start.1) | copy-done | bytes 262168
  2.5 61.0 %shard_map.41 = (f32[32,16,128]{2,1,0:T(8,128)S(1)}, f32[32,16,128]{2,1,0:T(8,128)S(1)}) custom-call(f32[32,16,128]{2,1,0:T(8,128)S(1)} %copy-done, f32[32,16,128]{2,1,0:T(8,128)S(1)} %copy-done.1), custom_call_target="tpu_custom_call" | custom-call | tf_op jit(solution)/shard_map/pallas_call | solution.py:742
  63.6 0.7 %copy.6 = f32[32,16,128]{2,1,0:T(8,128)} copy(f32[32,16,128]{2,1,0:T(8,128)S(1)} %get-tuple-element.4) | data formatting | bytes 524288
  64.3 0.7 %copy.7 = f32[32,16,128]{2,1,0:T(8,128)} copy(f32[32,16,128]{2,1,0:T(8,128)S(1)} %get-tuple-element.5) | data formatting | bytes 524288
Async XLA Ops:
  0.6 1.0 %copy-start = (f32[32,16,128]{2,1,0:T(8,128)S(1)}, f32[32,16,128]{2,1,0:T(8,128)}, u32[]{:S(2)}) copy-start(f32[32,16,128]{2,1,0:T(8,128)} %b_ref.1) | copy-start | bytes 786436
  1.6 0.9 %copy-start.1 = (f32[32,16,128]{2,1,0:T(8,128)S(1)}, f32[32,16,128]{2,1,0:T(8,128)}, u32[]{:S(2)}) copy-start(f32[32,16,128]{2,1,0:T(8,128)} %k_ref.1) | copy-start | bytes 786436

commit v4 on v3

--- a/solution.py
+++ b/solution.py
@@ -14,7 +14,7 @@
 DEEP = 4
 HALO = 4
 OFFSETS = [(i, j, k) for i in (-1, 0, 1) for j in (-1, 0, 1) for k in (-1, 0, 1) if i or j or k]
-EDGES = [offset for offset in OFFSETS if offset[2]]
+EDGES = sorted((offset for offset in OFFSETS if offset[2]), key=lambda offset: -sum(map(abs, offset)))
 
 
 def chebyshev_factors(sweeps):
@@ -71,13 +71,27 @@
     def groups(self, skip=0):
         skip = skip * self.pitch if self.h > 1 else 0
         first, last = skip, self.n - skip
-        count = -(-(last - first) // 96)
+        count = -(-(last - first) // 144)
         size = up8(-(-(last - first) // count))
         return [(lo, min(size, last - lo)) for lo in range(first, last, size)]
 
 
-def dot(a, b):
-    return jnp.dot(a, b, precision=lax.Precision.HIGHEST, preferred_element_type=jnp.float32)
+def thirds(value):
+    high = value.astype(jnp.bfloat16)
+    rest = value - high.astype(jnp.float32)
+    middle = rest.astype(jnp.bfloat16)
+    return (rest - middle.astype(jnp.float32)).astype(jnp.bfloat16), middle, high
+
+
+def dot(a, b, exact_left=False):
+    if exact_left:
+        left = a.astype(jnp.bfloat16)
+        pairs = [(left, part) for part in thirds(b)]
+    else:
+        right = b.astype(jnp.bfloat16)
+        pairs = [(part, right) for part in thirds(a)]
+    low, middle, high = (jnp.dot(x, y, preferred_element_type=jnp.float32) for x, y in pairs)
+    return (low + middle) + high
 
 
 def iota(shape, dim):
@@ -699,7 +713,7 @@
         cell_x, cell_y = gx * cx - reach + plane, gy * cy - reach + (row - plane * pitch)
         inside = (cell_x >= 0) & (cell_x < three.nx) & (cell_y >= 0) & (cell_y < three.ny)
         wanted = three.row(0, 0) + cell_x * three.pitch + cell_y
-        window = dot(jnp.where(inside & (source == wanted), 1.0, 0.0), field[...])
+        window = dot(jnp.where(inside & (source == wanted), 1.0, 0.0), field[...], True)
         weights = stretch(columns(last) + gz * last.nz, three.zo)
         prolong(picked, pitch, reach * pitch + reach, dot(window, weights), last, ref[2, "v"])
         lift(last)

time: 65.1 us -> 64.4 us (0.989)
    pallas_call x1, Pallas kernels: 61 us -> 60.4 us  [on_device(): pl.pallas_call(kernel, out_shape=(out, out), in_specs=[pl.BlockSpec(memor...]
where the time goes in v4:
time: 64.4 us; the launch traced here: 64.3 us
  Pallas kernels  60.4 us (94%)
  local copies, waits for them, and re-layouts  3.3 us (5%)
  between operations  0.65 us (1%)
    pallas_call x1, Pallas kernels, on_device(): pl.pallas_call(kernel, out_shape=(out, out), in_specs=[pl.BlockSpec(memor...  60.4 us
    unnamed x6, local copies, waits for them, and re-layouts  3.3 us

profile of v4, /device:TPU:1, one launch (start us, length us, event | category | flops | bytes accessed | tf_op | source)
XLA Modules:
  0.0 64.3 jit_solution(11959953728874898579)
XLA Ops:
  0.6 0.0 copy-start
  0.6 0.9 %copy-done = f32[32,16,128]{2,1,0:T(8,128)S(1)} copy-done((f32[32,16,128]{2,1,0:T(8,128)S(1)}, f32[32,16,128]{2,1,0:T(8,128)}, u32[]{:S(2)}) %copy-start) | copy-done | bytes 262168
  1.6 0.0 copy-start.1
  1.6 0.9 %copy-done.1 = f32[32,16,128]{2,1,0:T(8,128)S(1)} copy-done((f32[32,16,128]{2,1,0:T(8,128)S(1)}, f32[32,16,128]{2,1,0:T(8,128)}, u32[]{:S(2)}) %copy-start.1) | copy-done | bytes 262168
  2.5 60.4 %shard_map.41 = (f32[32,16,128]{2,1,0:T(8,128)S(1)}, f32[32,16,128]{2,1,0:T(8,128)S(1)}) custom-call(f32[32,16,128]{2,1,0:T(8,128)S(1)} %copy-done, f32[32,16,128]{2,1,0:T(8,128)S(1)} %copy-done.1), custom_call_target="tpu_custom_call" | custom-call | tf_op jit(solution)/shard_map/pallas_call | solution.py:756
  62.9 0.7 %copy.6 = f32[32,16,128]{2,1,0:T(8,128)} copy(f32[32,16,128]{2,1,0:T(8,128)S(1)} %get-tuple-element.4) | data formatting | bytes 524288
  63.6 0.7 %copy.7 = f32[32,16,128]{2,1,0:T(8,128)} copy(f32[32,16,128]{2,1,0:T(8,128)S(1)} %get-tuple-element.5) | data formatting | bytes 524288
Async XLA Ops:
  0.6 1.0 %copy-start = (f32[32,16,128]{2,1,0:T(8,128)S(1)}, f32[32,16,128]{2,1,0:T(8,128)}, u32[]{:S(2)}) copy-start(f32[32,16,128]{2,1,0:T(8,128)} %b_ref.1) | copy-start | bytes 786436
  1.6 0.9 %copy-start.1 = (f32[32,16,128]{2,1,0:T(8,128)S(1)}, f32[32,16,128]{2,1,0:T(8,128)}, u32[]{:S(2)}) copy-start(f32[32,16,128]{2,1,0:T(8,128)} %k_ref.1) | copy-start | bytes 786436

commit v5 on v4

--- a/solution.py
+++ b/solution.py
@@ -141,6 +141,8 @@
         ref = {key: value for key, value in zip(names, scratch)}
         gx, gy, gz = lax.axis_index("gx"), lax.axis_index("gy"), lax.axis_index("gz")
         plane_peers = [(i, j) for i in range(gxn) for j in range(gyn) if i or j]
+        plane_peers.sort(key=lambda peer: -min(peer[0], gxn - peer[0]) - 0.5 * min(peer[1], gyn - peer[1]))
+        depth_peers = sorted(range(1, gzn), key=lambda k: -min(k, gzn - k))
 
         def plane_peer(i, j):
             return lax.rem(gx + i, gxn), lax.rem(gy + j, gyn)
@@ -156,12 +158,6 @@
             fetch.start()
 
         barrier = pltpu.get_barrier_semaphore()
-        for i, j in plane_peers:
-            px, py = plane_peer(i, j)
-            pl.semaphore_signal(barrier, inc=1, device_id=(px, py, gz), device_id_type=MESH)
-        for k in range(1, gzn):
-            pl.semaphore_signal(barrier, inc=1, device_id=(gx, gy, depth_peer(k)), device_id_type=MESH)
-
         counters = [0, 0, 0]
         first, middle, last = local
         at = (gx, gy, gz)
@@ -182,9 +178,12 @@
             return tuple(at[a] + offset[a] for a in range(3))
 
         diagonal = [offset for offset in EDGES if offset[0] or offset[1]]
-        for offset in diagonal:
-            around_edge = tuple(lax.rem(at[a] + offset[a] + sizes[a], sizes[a]) for a in range(3))
-            pl.semaphore_signal(barrier, inc=1, device_id=around_edge, device_id_type=MESH)
+        for k in depth_peers:
+            pl.semaphore_signal(barrier, inc=1, device_id=(gx, gy, depth_peer(k)), device_id_type=MESH)
+        greeted = [(*plane_peer(i, j), gz) for i, j in plane_peers]
+        around_edge = [tuple(lax.rem(at[a] + o[a] + sizes[a], sizes[a]) for a in range(3)) for o in diagonal]
+        for place in greeted[:16] + around_edge + greeted[16:]:
+            pl.semaphore_signal(barrier, inc=1, device_id=place, device_id_type=MESH)
 
         for lv in (three, four):
             for name in ("d0", "d1", "v", "w"):
@@ -571,7 +570,7 @@
 
         def gather_depth_start(which, block):
             ref[None, "zs"][which] = block[:blk]
-            for k in range(1, gzn):
+            for k in depth_peers:
                 depth_copy(which, k).start()
 
         def gather_plane_start(which):

time: 64.4 us -> 63.6 us (0.988)
  Pallas kernels: 60.4 us -> 59.5 us
    pallas_call x1, Pallas kernels: 60.4 us -> 59.5 us  [on_device(): pl.pallas_call(kernel, out_shape=(out, out), in_specs=[pl.BlockSpec(memor...]
where the time goes in v5:
time: 63.6 us; the launch traced here: 63.4 us
  Pallas kernels  59.5 us (94%)
  local copies, waits for them, and re-layouts  3.3 us (5%)
  between operations  0.65 us (1%)
    pallas_call x1, Pallas kernels, on_device(): pl.pallas_call(kernel, out_shape=(out, out), in_specs=[pl.BlockSpec(memor...  59.5 us
    unnamed x6, local copies, waits for them, and re-layouts  3.3 us

profile of v5, /device:TPU:1, one launch (start us, length us, event | category | flops | bytes accessed | tf_op | source)
XLA Modules:
  0.0 63.4 jit_solution(6202069645095799702)
XLA Ops:
  0.6 0.0 copy-start
  0.6 0.9 %copy-done = f32[32,16,128]{2,1,0:T(8,128)S(1)} copy-done((f32[32,16,128]{2,1,0:T(8,128)S(1)}, f32[32,16,128]{2,1,0:T(8,128)}, u32[]{:S(2)}) %copy-start) | copy-done | bytes 262168
  1.6 0.0 copy-start.1
  1.6 0.9 %copy-done.1 = f32[32,16,128]{2,1,0:T(8,128)S(1)} copy-done((f32[32,16,128]{2,1,0:T(8,128)S(1)}, f32[32,16,128]{2,1,0:T(8,128)}, u32[]{:S(2)}) %copy-start.1) | copy-done | bytes 262168
  2.5 59.5 %shard_map.41 = (f32[32,16,128]{2,1,0:T(8,128)S(1)}, f32[32,16,128]{2,1,0:T(8,128)S(1)}) custom-call(f32[32,16,128]{2,1,0:T(8,128)S(1)} %copy-done, f32[32,16,128]{2,1,0:T(8,128)S(1)} %copy-done.1), custom_call_target="tpu_custom_call" | custom-call | tf_op jit(solution)/shard_map/pallas_call | solution.py:755
  62.0 0.7 %copy.6 = f32[32,16,128]{2,1,0:T(8,128)} copy(f32[32,16,128]{2,1,0:T(8,128)S(1)} %get-tuple-element.4) | data formatting | bytes 524288
  62.7 0.7 %copy.7 = f32[32,16,128]{2,1,0:T(8,128)} copy(f32[32,16,128]{2,1,0:T(8,128)S(1)} %get-tuple-element.5) | data formatting | bytes 524288
Async XLA Ops:
  0.6 1.0 %copy-start = (f32[32,16,128]{2,1,0:T(8,128)S(1)}, f32[32,16,128]{2,1,0:T(8,128)}, u32[]{:S(2)}) copy-start(f32[32,16,128]{2,1,0:T(8,128)} %b_ref.1) | copy-start | bytes 786436
  1.6 0.9 %copy-start.1 = (f32[32,16,128]{2,1,0:T(8,128)S(1)}, f32[32,16,128]{2,1,0:T(8,128)}, u32[]{:S(2)}) copy-start(f32[32,16,128]{2,1,0:T(8,128)} %k_ref.1) | copy-start | bytes 786436
